TPU v7x, 32 devices: a whole 2x2x4 slice. The times are simulated.
32 devices in a mesh: wide: 8 (over z, x), narrow: 4 (over y, core).
Axes of the slice: x: 2, y: 2, z: 4, core: 2. Of those that a mesh axis runs over, the one named last changes fastest.
Arguments:
- tokens: bfloat16 [4096, 2048], P(('wide', 'narrow')), may hold values from -6 to 6
- expert_ids: int32 [4096], P(('wide', 'narrow')), may hold values from 0 to 3, as said below
- route_weights: float32 [4096], P(('wide', 'narrow')), may hold values from 0.2 to 1
- out_grad: bfloat16 [4096, 2048], P(('wide', 'narrow')), may hold values from -0.796875 to 0.796875
- w_gate_up: bfloat16 [32, 2048, 256], P(('wide', 'narrow')), may hold values from -0.125 to 0.125
- w_down: bfloat16 [32, 128, 2048], P(('wide', 'narrow')), may hold values from -0.375 to 0.375
- second_moment: bfloat16 [32, 128, 2048], P(('wide', 'narrow')), may hold values from 0.0049743652 to 0.099609375
Outputs:
- grad_gate_up: bfloat16 [32, 2048, 256], P(('wide', 'narrow'))
- down_update: bfloat16 [32, 128, 2048], P(('wide', 'narrow'))
Inputs may be any that keep to these rules, and one draw needn't show every extreme that they name: `expert_ids`: values below 2 name the token's own group's experts, the others the next group's. Within the rows of one device no value appears more than 48 times; in every group of 4 devices along narrow one value appears exactly 48 times on every device of the group.
All inputs are finite; a program needn't handle non-finite values.
Results may differ from a plain program's by a relative error of at most 0.0066.
Values may be sent and summed in bfloat16 or wider, within the bound.
A program may use at most 64 MiB of HBM per device.

v0:
```python
import functools

import jax
import jax.numpy as jnp
from jax import lax
from jax.experimental import pallas as pl
from jax.experimental.pallas import tpu as pltpu
from jax.sharding import PartitionSpec as P

second_correction = 1.0 - 0.95**10
bf16 = jnp.bfloat16
f32 = jnp.float32
LIMIT = 32 * 1024 * 1024


def mm(a, b, dims):
    return lax.dot_general(a, b, (dims, ((), ())), preferred_element_type=f32)


def kernel(
    groups, wides, cap, slot, chunks,
    ids_hbm, rw_hbm, tok_hbm, og_hbm, wgu_hbm, wdn_hbm, sm_hbm,
    acc_p, rows_last, pre_last, ustage,
    ids, rw, tok, og, wgu, wdn, sm, px, pd, rx, rd, pre, hid, acc_d,
    in_sem, sx, rxs, sd, rds, sc, rcs, fsx, frx, fsd, frd, fsc, frc,
):
    half = groups // 2
    width = tok.shape[1]
    hidden_units = wdn.shape[0]
    wide = lax.axis_index("wide")
    narrow = lax.axis_index("narrow")
    home = narrow // 2
    parity = lax.rem(narrow, 2)
    ahead = lax.rem(wide + 1, wides)
    behind = lax.rem(wide + wides - 1, wides)

    def device(w, n):
        return {"wide": w, "narrow": n}

    def expert_at(j):
        return lax.rem(home + j, half)

    sibling = device(wide, 2 * home + 1 - parity)

    order = [(0, 0), (1, 0)] + [(0, j) for j in range(1, half)] + [(1, j) for j in range(1, half)]
    early = 2 + (half - 1)
    late = half - 1
    remote_early = list(range(2, early)) + [1]
    late_list = list(range(early, early + late))

    loads = []
    for i, (src, dst) in enumerate(
        (
            (tok_hbm, tok), (og_hbm, og), (wgu_hbm.at[0], wgu), (wdn_hbm.at[0], wdn),
            (sm_hbm.at[0], sm), (ids_hbm, ids), (rw_hbm, rw),
        )
    ):
        copy = pltpu.make_async_copy(src, dst, in_sem.at[i])
        loads.append(copy)
    for i in (5, 0, 6, 1, 2, 3, 4):
        loads[i].start()

    barrier = pltpu.get_barrier_semaphore()
    partners = [device(behind, 2 * expert_at(j) + parity) for j in range(half)]
    partners += [device(wide, 2 * expert_at(j) + parity) for j in range(1, half)]
    partners.append(sibling)
    for partner in partners:
        pl.semaphore_signal(barrier, inc=1, device_id=partner, device_id_type=pl.DeviceIdType.MESH)

    loads[5].wait()
    loads[6].wait()
    count = tok.shape[0]
    labels = ids[...]
    pad_groups = max(8, groups)
    onehot = (lax.broadcasted_iota(jnp.int32, (pad_groups, count), 0) == labels).astype(f32)
    before = (
        lax.broadcasted_iota(jnp.int32, (count, count), 0)
        < lax.broadcasted_iota(jnp.int32, (count, count), 1)
    ).astype(f32)
    counted = mm(onehot.astype(bf16), before.astype(bf16), ((1,), (0,)))
    within = jnp.sum(counted * onehot, axis=0, keepdims=True).astype(jnp.int32)
    weights = rw[...]
    slots = lax.broadcasted_iota(jnp.int32, (slot, count), 0)

    def select_of(b):
        kind, j = order[b]
        value = kind * half + expert_at(j)
        return jnp.logical_and(labels == value, slots == within)

    def rows(b, h):
        return pl.ds((2 * b + h) * slot, slot)

    def dest(b):
        kind, j = order[b]
        return device(ahead if kind else wide, 2 * expert_at(j) + parity)

    def remote(src, dst, s, r, dev):
        return pltpu.make_async_remote_copy(
            src_ref=src, dst_ref=dst, send_sem=s, recv_sem=r,
            device_id=dev, device_id_type=pl.DeviceIdType.MESH,
        )

    part = width // chunks

    def send_x(b):
        return remote(px.at[b], rx.at[rows(b, 0)], sx.at[b], rxs.at[b], dest(b))

    def send_d(b):
        return remote(pd.at[b], rd.at[rows(b, 0)], sd.at[b], rds.at[b], dest(b))

    def send_c(b, c):
        cols = pl.ds(c * part, part)
        i = (b - early) * chunks + c
        return remote(
            pd.at[b, :, cols], rd.at[rows(b, 0), cols], sc.at[i], rcs.at[i], dest(b)
        )

    def forward_x(b):
        return remote(rx.at[rows(b, 0)], rx.at[rows(b, 1)], fsx.at[b], frx.at[b], sibling)

    def forward_d(b):
        return remote(rd.at[rows(b, 0)], rd.at[rows(b, 1)], fsd.at[b], frd.at[b], sibling)

    def forward_c(b, c):
        cols = pl.ds(c * part, part)
        i = (b - early) * chunks + c
        return remote(
            rd.at[rows(b, 0), cols], rd.at[rows(b, 1), cols], fsc.at[i], frc.at[i], sibling
        )

    started = []

    def go(copy):
        copy.start()
        started.append(copy)

    def pack_x(b):
        return mm(select_of(b).astype(f32).astype(bf16), tok[...], ((1,), (0,))).astype(bf16)

    def pack_d(b):
        select = select_of(b)
        weight = jnp.sum(jnp.where(select, weights, 0.0), axis=1, keepdims=True)
        placed = mm(select.astype(f32).astype(bf16), og[...], ((1,), (0,)))
        return (weight * placed).astype(bf16)

    loads[0].wait()
    for b in remote_early:
        px[b] = pack_x(b)
    pl.semaphore_wait(barrier, len(partners))
    for b in remote_early:
        go(send_x(b))
    loads[1].wait()
    for b in remote_early:
        pd[b] = pack_d(b)
    for b in late_list:
        px[b] = pack_x(b)
    for b in remote_early:
        go(send_d(b))
    for b in late_list:
        go(send_x(b))
    for b in late_list:
        pd[b] = pack_d(b)
    rx[rows(0, 0), :] = pack_x(0)
    for b in late_list:
        for c in range(chunks):
            go(send_c(b, c))
    rd[rows(0, 0), :] = pack_d(0)
    go(forward_x(0))
    go(forward_d(0))
    loads[2].wait()
    loads[3].wait()

    def project(r):
        projected = mm(rx[r, :], wgu[...], ((1,), (0,)))
        gate_pre = projected[:, :hidden_units]
        up_pre = projected[:, hidden_units:]
        logistic = jax.nn.sigmoid(gate_pre)
        swished = gate_pre * logistic
        hid[r, :] = (swished * up_pre).astype(bf16)
        return up_pre * logistic * (1.0 + gate_pre * (1.0 - logistic)), swished

    def finish(target, r, hidden_grad, factors):
        target[r, :] = jnp.concatenate(
            [hidden_grad * factors[0], hidden_grad * factors[1]], axis=1
        ).astype(bf16)

    for b in remote_early:
        send_x(b).wait_recv()
        go(forward_x(b))
    for b in remote_early:
        send_d(b).wait_recv()
        go(forward_d(b))
    for b in range(early):
        forward_x(b).wait_recv()
        forward_d(b).wait_recv()
    first = pl.ds(0, early * 2 * slot)
    finish(pre, first, mm(rd[first, :], wdn[...], ((1,), (1,))), project(first))
    for i in range(width // 256):
        cols = pl.ds(i * 256, 256)
        acc_p[cols, :] = mm(rx[first, cols], pre[first, :], ((0,), (0,)))
        acc_d[:, cols] = mm(hid[first, :], rd[first, cols], ((0,), (0,)))

    for b in late_list:
        send_x(b).wait_recv()
        go(forward_x(b))
    for b in late_list:
        forward_x(b).wait_recv()
    last = pl.ds(early * 2 * slot, late * 2 * slot)
    factors = project(last)
    rows_last[...] = rx[last, :]
    loads[4].wait()
    hidden_grad = jnp.zeros((late * 2 * slot, hidden_units), f32)

    def relay(c):
        for b in late_list:
            send_c(b, c).wait_recv()
            go(forward_c(b, c))

    relay(0)
    for c in range(chunks):
        if c + 1 < chunks:
            relay(c + 1)
        for b in late_list:
            forward_c(b, c).wait_recv()
        cols = pl.ds(c * part, part)
        hidden_grad = hidden_grad + mm(rd[last, cols], wdn[:, cols], ((1,), (1,)))
        total = acc_d[:, cols] + mm(hid[last, :], rd[last, cols], ((0,), (0,)))
        second = 0.95 * sm[:, cols].astype(f32) + 0.05 * total * total
        update = total / (jnp.sqrt(second / second_correction) + 1e-08)
        ustage[:, cols] = (update + 0.1 * wdn[:, cols].astype(f32)).astype(bf16)

    finish(pre_last, slice(None), hidden_grad, factors)
    for copy in started:
        copy.wait_send()


def final_kernel(acc_p, rows_last, pre_last, update, gout, uout, gstage, out_sem):
    tiles = acc_p.shape[0] // 256
    outs = [pltpu.make_async_copy(update, uout.at[0], out_sem.at[tiles])]
    outs[0].start()
    for i in range(tiles):
        r = pl.ds(i * 256, 256)
        gstage[r, :] = (acc_p[r, :] + mm(rows_last[:, r], pre_last[...], ((0,), (0,)))).astype(bf16)
        copy = pltpu.make_async_copy(gstage.at[r], gout.at[0, r], out_sem.at[i])
        copy.start()
        outs.append(copy)
    for copy in outs:
        copy.wait()


def body(tokens, expert_ids, route_weights, out_grad, w_gate_up, w_down, second_moment):
    groups = lax.axis_size("narrow")
    wides = lax.axis_size("wide")
    count, width = tokens.shape
    cap = 3 * count // (2 * groups)
    slot = -(-cap // 16) * 16
    chunks = 4
    columns = w_gate_up.shape[2]
    units = w_down.shape[1]
    all_rows = groups * 2 * slot
    late = groups // 2 - 1
    dma = pltpu.SemaphoreType.DMA
    any_spec = pl.BlockSpec(memory_space=pl.ANY)
    vmem_spec = pl.BlockSpec(memory_space=pltpu.VMEM)
    last_rows = late * 2 * slot
    held = pl.pallas_call(
        functools.partial(kernel, groups, wides, cap, slot, chunks),
        out_shape=(
            pltpu.VMEM((width, columns), f32),
            pltpu.VMEM((last_rows, width), bf16),
            pltpu.VMEM((last_rows, columns), bf16),
            pltpu.VMEM((units, width), bf16),
        ),
        in_specs=[any_spec] * 7,
        out_specs=(vmem_spec,) * 4,
        scratch_shapes=[
            pltpu.VMEM((1, count), jnp.int32),
            pltpu.VMEM((1, count), f32),
            pltpu.VMEM((count, width), bf16),
            pltpu.VMEM((count, width), bf16),
            pltpu.VMEM((width, columns), bf16),
            pltpu.VMEM((units, width), bf16),
            pltpu.VMEM((units, width), bf16),
            pltpu.VMEM((groups, slot, width), bf16),
            pltpu.VMEM((groups, slot, width), bf16),
            pltpu.VMEM((all_rows, width), bf16),
            pltpu.VMEM((all_rows, width), bf16),
            pltpu.VMEM((all_rows, columns), bf16),
            pltpu.VMEM((all_rows, units), bf16),
            pltpu.VMEM((units, width), f32),
            dma((7,)),
            dma((groups,)), dma((groups,)), dma((groups,)), dma((groups,)),
            dma((late * chunks,)), dma((late * chunks,)),
            dma((groups,)), dma((groups,)), dma((groups,)), dma((groups,)),
            dma((late * chunks,)), dma((late * chunks,)),
        ],
        compiler_params=pltpu.CompilerParams(
            collective_id=0, has_side_effects=True, vmem_limit_bytes=LIMIT
        ),
    )(
        *(
            pltpu.with_memory_space_constraint(value, pltpu.HBM)
            for value in (
                expert_ids.reshape(1, count), route_weights.reshape(1, count),
                tokens, out_grad, w_gate_up, w_down, second_moment,
            )
        ),
    )
    return pl.pallas_call(
        final_kernel,
        out_shape=(
            jax.ShapeDtypeStruct((1, width, columns), bf16),
            jax.ShapeDtypeStruct((1, units, width), bf16),
        ),
        in_specs=[vmem_spec] * 4,
        out_specs=(any_spec, any_spec),
        scratch_shapes=[pltpu.VMEM((width, columns), bf16), dma((width // 256 + 1,))],
        compiler_params=pltpu.CompilerParams(vmem_limit_bytes=LIMIT),
    )(*held)


def solution(mesh):
    placed = (
        P(("wide", "narrow"), None),
        P(("wide", "narrow")),
        P(("wide", "narrow")),
        P(("wide", "narrow"), None),
        P(("wide", "narrow"), None, None),
        P(("wide", "narrow"), None, None),
        P(("wide", "narrow"), None, None),
    )
    return jax.shard_map(
        body,
        mesh=mesh,
        in_specs=placed,
        out_specs=(P(("wide", "narrow"), None, None), P(("wide", "narrow"), None, None)),
        check_vma=False,
    )
```

profile of v0, /device:TPU:1, one launch (start us, length us, event | category | flops | bytes accessed | tf_op | source)
XLA Modules:
  0.0 29.4 jit_solution(9734368626778387471)
XLA Ops:
  0.6 27.5 %shard_map.86 = (f32[2048,256]{1,0:T(8,128)S(1)}, bf16[96,2048]{1,0:T(8,128)(2,1)S(1)}, bf16[96,256]{1,0:T(8,128)(2,1)S(1)}, bf16[128,2048]{1,0:T(8,128)(2,1)S(1)}) custom-call(s32[1,128]{1,0:T(1,128)} %bitcast.2, f32[1,128]{1,0:T(1,128)} %bitcast.3, bf16[128,2048]{1,0:T(8,128)(2,1)} %tok_hbm.1, bf16[128,2048]{1,0:T(8,128)(2,1)} %og_hbm.1, ...), custom_call_target="tpu_custom_call" | custom-call | tf_op jit(solution)/shard_map/pallas_call | solution.py:266
  28.1 1.3 %shard_map.87 = (bf16[1,2048,256]{2,1,0:T(8,128)(2,1)}, bf16[1,128,2048]{2,1,0:T(8,128)(2,1)}) custom-call(f32[2048,256]{1,0:T(8,128)S(1)} %get-tuple-element.6.acc_p, bf16[96,2048]{1,0:T(8,128)(2,1)S(1)} %get-tuple-element.7.rows_last, bf16[96,256]{1,0:T(8,128)(2,1)S(1)} %get-tuple-element.8.pre_last, bf16[128,2048]{1,0:T(8,128)(2,1)S(1)} %get-tuple-element.9.update), custom_call_target="tpu_custom_call" | custom-call | tf_op jit(solution)/shard_map/pallas_call | solution.py:309
where the time goes:
time: 29.9 us; the launch traced here: 29.4 us
  Pallas kernels  28.8 us (96%)
  between operations  0.64 us (2%)
    pallas_call x1, Pallas kernels, body(): pl.pallas_call(functools.partial(kernel, groups, wides, cap, slot, chunks...  27.5 us
    pallas_call x1, Pallas kernels, body(): pl.pallas_call(final_kernel, out_shape=(jax.ShapeDtypeStruct((1, width, c...  1.3 us

commit v1 on v0

v1 whole, which is shorter than its diff:
```python
import functools

import jax
import jax.numpy as jnp
from jax import lax
from jax.experimental import pallas as pl
from jax.experimental.pallas import tpu as pltpu
from jax.sharding import PartitionSpec as P

second_correction = 1.0 - 0.95**10
bf16 = jnp.bfloat16
f32 = jnp.float32
LIMIT = 32 * 1024 * 1024


def mm(a, b, dims):
    return lax.dot_general(a, b, (dims, ((), ())), preferred_element_type=f32)


RELAYED = True
LENDS = 2
GATE = 1
PACK = (2, 3, 3)
FIRST_X = (2, 3, 3)
EARLY_D = (5, 3)
DIAGONAL_X = (4, 4)
LATE_D = (2, 2, 2, 1, 1)


def spans(width, weights):
    unit = width // sum(weights)
    out, at = [], 0
    for weight in weights:
        out.append((at * unit, weight * unit))
        at += weight
    return out


def kernel(
    groups, wides, slot, relayed,
    ids_hbm, rw_hbm, tok_hbm, og_hbm, wgu_hbm, wdn_hbm, sm_hbm,
    acc_p, turned, pre_last, ustage,
    ids, rw, tok, og, wgu, wdn, sm, px, pd, rx, rd, lent, pre, hid, acc_d, moment, decay,
    in_sem, send_sem, recv_sem, lent_sem, pass_sem, fsend_sem, frecv_sem, twice_sem, ready_sem,
):
    half = groups // 2
    width = tok.shape[1]
    hidden_units = wdn.shape[0]
    wide = lax.axis_index("wide")
    narrow = lax.axis_index("narrow")
    home = narrow // 2
    parity = lax.rem(narrow, 2)

    def along(step):
        return lax.rem(wide + wides + step, wides)

    def device(w, n):
        return {"wide": w, "narrow": n}

    def peer(j):
        return 2 * lax.rem(home + j, half) + parity

    odd = lax.rem(wide, 2) == 1
    even = jnp.logical_not(odd)
    sibling = device(wide, 2 * home + 1 - parity)

    order = [(0, 0), (1, 0)] + [(0, j) for j in range(2, half)]
    order += [(1, j) for j in range(1, half)] + [(0, 1)]
    early = list(range(half))
    late = list(range(half, groups))
    direct = 1
    diagonal = [b for b in late if order[b][0]]
    beside = [b for b in range(1, groups) if not order[b][0]]

    loads = []
    for i, (src, dst) in enumerate(
        (
            (tok_hbm, tok), (og_hbm, og), (wgu_hbm.at[0], wgu), (wdn_hbm.at[0], wdn),
            (sm_hbm.at[0], sm), (ids_hbm, ids), (rw_hbm, rw),
        )
    ):
        loads.append(pltpu.make_async_copy(src, dst, in_sem.at[i]))
    for i in (5, 0, 6, 1):
        loads[i].start()

    barrier = pltpu.get_barrier_semaphore()

    def signal(sem, partner):
        pl.semaphore_signal(sem, inc=1, device_id=partner, device_id_type=pl.DeviceIdType.MESH)

    signal(barrier, device(along(-1), narrow))
    for j in range(1, half):
        signal(barrier, device(wide, peer(j)))
    signal(barrier, sibling)
    if relayed:

        @pl.when(even)
        def _():
            signal(barrier, device(along(1), narrow))

    loads[5].wait()
    count = tok.shape[0]
    labels = ids[...]
    pad_groups = max(8, groups)
    onehot = (lax.broadcasted_iota(jnp.int32, (pad_groups, count), 0) == labels).astype(f32)
    before = (
        lax.broadcasted_iota(jnp.int32, (count, count), 0)
        < lax.broadcasted_iota(jnp.int32, (count, count), 1)
    ).astype(f32)
    counted = mm(onehot.astype(bf16), before.astype(bf16), ((1,), (0,)))
    within = jnp.sum(counted * onehot, axis=0, keepdims=True).astype(jnp.int32)
    slots = lax.broadcasted_iota(jnp.int32, (slot, count), 0)

    def select_of(b):
        kind, j = order[b]
        value = kind * half + lax.rem(home + j, half)
        return jnp.logical_and(labels == value, slots == within)

    def rows(b, h):
        return pl.ds((2 * b + h) * slot, slot)

    def remote(src, dst, s, r, dev):
        return pltpu.make_async_remote_copy(
            src_ref=src, dst_ref=dst, send_sem=s, recv_sem=r,
            device_id=dev, device_id_type=pl.DeviceIdType.MESH,
        )

    index, parts = {}, {}
    for b in range(1, groups):
        widths = (DIAGONAL_X if b in diagonal else FIRST_X, EARLY_D if b in early else LATE_D)
        for a in (0, 1):
            parts[b, a] = spans(width, widths[a])
            for c in range(len(parts[b, a])):
                index[b, a, c] = len(index)
    packed, received = (px, pd), (rx, rd)

    def cols_of(b, a, c):
        return pl.ds(*parts[b, a][c])

    def send(b, a, c):
        kind, j = order[b]
        cols = cols_of(b, a, c)
        return remote(
            packed[a].at[b - 1, :, cols], received[a].at[rows(b, 0), cols],
            send_sem.at[2 if a == 0 and b == direct and c < lends else a], recv_sem.at[index[b, a, c]], device(along(kind), peer(j)),
        )

    lends = LENDS if relayed else 0

    def lend(c):
        cols = cols_of(direct, 0, c)
        return remote(
            px.at[direct - 1, :, cols], lent.at[:, cols],
            send_sem.at[2], lent_sem.at[c], device(along(-1), narrow),
        )

    def hand_on(c):
        cols = cols_of(direct, 0, c)
        return remote(
            lent.at[:, cols], rx.at[rows(direct, 0), cols],
            pass_sem.at[0], recv_sem.at[index[direct, 0, c]], device(along(2), narrow),
        )

    def go_first(c):
        if relayed:

            @pl.when(odd)
            def _():
                lend(c).start()

            @pl.when(even)
            def _():
                send(direct, 0, c).start()
        else:
            send(direct, 0, c).start()

    def go_rest():
        for c in range(lends, len(FIRST_X)):
            send(direct, 0, c).start()
        for c in range(len(parts[direct, 1])):
            send(direct, 1, c).start()
        for a in (0, 1):
            for b in diagonal:
                for c in range(len(parts[b, a]) - a):
                    send(b, a, c).start()

    def first_sent():
        part = px.at[0, :, pl.ds(0, first_columns)]
        remote(part, part, send_sem.at[2], recv_sem.at[0], sibling).wait_send()

    held_back = jnp.logical_and(odd, wide != wides - 1)
    first_columns = sum(FIRST_X[:lends]) * width // sum(FIRST_X)

    final = len(LATE_D) - 1

    def send_twice(b):
        kind, j = order[b]
        cols, other = cols_of(b, 1, final), 2 * lax.rem(home + j, half) + 1 - parity
        return remote(
            pd.at[b - 1, :, cols], rd.at[rows(b, 1), cols],
            twice_sem.at[0], twice_sem.at[1 + b - half], device(along(kind), other),
        )

    def forward(b, a, c):
        cols = cols_of(b, a, c)
        which = a if b < half else 2 + (b in beside) if a == 0 else 4 + c
        return remote(
            received[a].at[rows(b, 0), cols], received[a].at[rows(b, 1), cols],
            fsend_sem.at[a], frecv_sem.at[which], sibling,
        )

    def settle(which, a, blocks, cols=slice(None)):
        part = received[a].at[pl.ds(0, blocks * slot), cols]
        remote(part, part, fsend_sem.at[a], frecv_sem.at[which], sibling).wait_recv()

    selects = [select_of(b) for b in range(groups)]
    chosen = jnp.concatenate([s.astype(f32) for s in selects], axis=0).astype(bf16)

    def store(a, cols, block):
        for b in range(groups):
            piece = block[b * slot : (b + 1) * slot]
            if b:
                packed[a][b - 1, :, cols] = piece
            else:
                received[a][rows(0, 0), cols] = piece

    loads[0].wait()
    for i in (2, 3, 4):
        loads[i].start()
    for n, (start, size) in enumerate(spans(width, PACK)):
        cols = pl.ds(start, size)
        store(0, cols, mm(chosen, tok[:, cols], ((1,), (0,))).astype(bf16))
        if n == 0:
            near = 1 + half - 1 + 1
            if relayed:

                @pl.when(odd)
                def _():
                    pl.semaphore_wait(barrier, near + 1)

                @pl.when(even)
                def _():
                    pl.semaphore_wait(barrier, near)
            else:
                pl.semaphore_wait(barrier, near)
        for c, (at, extent) in enumerate(spans(width, FIRST_X)):
            if at + extent == start + size:
                if c < lends:
                    go_first(c)
                for b in beside:
                    send(b, 0, c).start()
        if n == 0:
            for j in range(1, half):
                signal(ready_sem, device(wide, peer(j)))
    loads[6].wait()
    weights = rw[...]
    weight = jnp.concatenate(
        [jnp.sum(jnp.where(s, weights, 0.0), axis=1, keepdims=True) for s in selects], axis=0
    )
    loads[1].wait()
    for start, size in spans(width, PACK):
        cols = pl.ds(start, size)
        placed = mm(chosen, og[:, cols], ((1,), (0,)))
        store(1, cols, (weight * placed).astype(bf16))
    for b in beside:
        for c in range(len(parts[b, 1]) - (b in late)):
            send(b, 1, c).start()
    if half > 1:
        pl.semaphore_wait(ready_sem, half - 1)
    if relayed:
        pl.when(jnp.logical_not(held_back))(go_rest)
    else:
        go_rest()
    for a in (0, 1):
        whole = received[a]
        remote(
            whole.at[rows(0, 0)], whole.at[rows(0, 1)],
            fsend_sem.at[a], frecv_sem.at[a], sibling,
        ).start()
    loads[2].wait()
    loads[3].wait()
    loads[4].wait()
    if relayed:

        @pl.when(even)
        def _():
            for c in range(lends):
                lend(c).wait_recv()
                hand_on(c).start()

    def project(r):
        projected = mm(rx[r, :], wgu[...], ((1,), (0,)))
        gate_pre = projected[:, :hidden_units]
        up_pre = projected[:, hidden_units:]
        logistic = jax.nn.sigmoid(gate_pre)
        swished = gate_pre * logistic
        hid[r, :] = (swished * up_pre).astype(bf16)
        return up_pre * logistic * (1.0 + gate_pre * (1.0 - logistic)), swished

    def finish(target, r, hidden_grad, factors):
        target[r, :] = jnp.concatenate(
            [hidden_grad * factors[0], hidden_grad * factors[1]], axis=1
        ).astype(bf16)

    def take(b, a, c):
        send(b, a, c).wait_recv()
        forward(b, a, c).start()

    def take_all(blocks, a):
        for b in blocks:
            for c in range(len(parts[b, a])):
                take(b, a, c)
                if relayed and (b, a, c) == (direct, 0, GATE):
                    pl.when(held_back)(go_rest)

    take_all(early[1:], 0)
    take_all([late[-1]], 0)
    settle(0, 0, half)
    settle(3, 0, 1)
    first = pl.ds(0, half * 2 * slot)
    last = pl.ds(half * 2 * slot, half * 2 * slot)
    factors_first = project(first)
    take_all(early[1:], 1)
    for b in late:
        send(b, 1, final).start()
        send_twice(b).start()
    moment[...] = (0.95 / second_correction) * sm[...].astype(f32)
    decay[...] = 0.1 * wdn[...].astype(f32)
    settle(1, 1, half)
    finish(pre, first, mm(rd[first, :], wdn[...], ((1,), (1,))), factors_first)
    for i in range(width // 256):
        cols = pl.ds(i * 256, 256)
        acc_p[cols, :] = mm(rx[first, cols], pre[first, :], ((0,), (0,)))
        acc_d[:, cols] = mm(hid[first, :], rd[first, cols], ((0,), (0,)))
    take_all(diagonal, 0)
    settle(2, 0, half - 1)
    factors = project(last)
    turned[...] = rx[last, :].T
    turned_hid = hid[last, :].T
    hidden_grad = jnp.zeros((half * 2 * slot, hidden_units), f32)
    late_d = spans(width, LATE_D)

    def relay(c):
        for b in late:
            take(b, 1, c)

    def add(c):
        cols = pl.ds(*late_d[c])
        return hidden_grad + mm(rd[last, cols], wdn[:, cols], ((1,), (1,)))

    def update(c):
        cols = pl.ds(*late_d[c])
        total = acc_d[:, cols] + mm(turned_hid, rd[last, cols], ((1,), (0,)))
        second = moment[:, cols] + (0.05 / second_correction) * total * total
        root = second * lax.rsqrt(second)
        ustage[:, cols] = (total / (root + 1e-08) + decay[:, cols]).astype(bf16)

    for c in range(final):
        relay(c)
    for c in range(final):
        settle(4 + c, 1, half, pl.ds(*late_d[c]))
        hidden_grad = add(c)
        update(c)
    for b in late:
        send(b, 1, final).wait_recv()
        send_twice(b).wait_recv()
    hidden_grad = add(final)
    finish(pre_last, slice(None), hidden_grad, factors)
    update(final)
    part = px.at[1:]
    remote(part, part, send_sem.at[0], recv_sem.at[0], sibling).wait_send()
    if relayed:
        first_sent()
        part = px.at[0, :, pl.ds(first_columns, width - first_columns)]
        remote(part, part, send_sem.at[0], recv_sem.at[0], sibling).wait_send()
    else:
        remote(px.at[0], px.at[0], send_sem.at[0], recv_sem.at[0], sibling).wait_send()
    remote(pd, pd, send_sem.at[1], recv_sem.at[0], sibling).wait_send()
    part = rx.at[pl.ds(0, groups * slot)]
    remote(part, part, fsend_sem.at[0], frecv_sem.at[0], sibling).wait_send()
    part, cols = rd.at[pl.ds(0, groups * slot)], pl.ds(0, late_d[final][0])
    rest = pl.ds(late_d[final][0], late_d[final][1])
    remote(part.at[:, cols], part.at[:, cols], fsend_sem.at[1], frecv_sem.at[0], sibling).wait_send()
    part = rd.at[pl.ds(0, half * slot), rest]
    remote(part, part, fsend_sem.at[1], frecv_sem.at[0], sibling).wait_send()
    remote(part, part, twice_sem.at[0], frecv_sem.at[0], sibling).wait_send()
    if relayed:

        @pl.when(even)
        def _():
            part = lent.at[:, pl.ds(0, first_columns)]
            remote(part, part, pass_sem.at[0], recv_sem.at[0], sibling).wait_send()


def final_kernel(acc_p, turned, pre_last, update, gout, uout, gstage, out_sem):
    tiles = acc_p.shape[0] // 256
    outs = [pltpu.make_async_copy(update, uout.at[0], out_sem.at[tiles])]
    outs[0].start()
    for i in range(tiles):
        r = pl.ds(i * 256, 256)
        gstage[r, :] = (acc_p[r, :] + mm(turned[r, :], pre_last[...], ((1,), (0,)))).astype(bf16)
        copy = pltpu.make_async_copy(gstage.at[r], gout.at[0, r], out_sem.at[i])
        copy.start()
        outs.append(copy)
    for copy in outs:
        copy.wait()


def body(tokens, expert_ids, route_weights, out_grad, w_gate_up, w_down, second_moment):
    groups = lax.axis_size("narrow")
    wides = lax.axis_size("wide")
    count, width = tokens.shape
    cap = 3 * count // (2 * groups)
    slot = -(-cap // 16) * 16
    columns = w_gate_up.shape[2]
    units = w_down.shape[1]
    half = groups // 2
    all_rows = groups * 2 * slot
    last_rows = half * 2 * slot
    relayed = RELAYED and wides % 2 == 0 and wides >= 4
    chunks = (groups - 1) * (len(FIRST_X) + len(LATE_D))
    dma = pltpu.SemaphoreType.DMA
    any_spec = pl.BlockSpec(memory_space=pl.ANY)
    vmem_spec = pl.BlockSpec(memory_space=pltpu.VMEM)
    held = pl.pallas_call(
        functools.partial(kernel, groups, wides, slot, relayed),
        out_shape=(
            pltpu.VMEM((width, columns), f32),
            pltpu.VMEM((width, last_rows), bf16),
            pltpu.VMEM((last_rows, columns), bf16),
            pltpu.VMEM((units, width), bf16),
        ),
        in_specs=[any_spec] * 7,
        out_specs=(vmem_spec,) * 4,
        scratch_shapes=[
            pltpu.VMEM((1, count), jnp.int32),
            pltpu.VMEM((1, count), f32),
            pltpu.VMEM((count, width), bf16),
            pltpu.VMEM((count, width), bf16),
            pltpu.VMEM((width, columns), bf16),
            pltpu.VMEM((units, width), bf16),
            pltpu.VMEM((units, width), bf16),
            pltpu.VMEM((groups - 1, slot, width), bf16),
            pltpu.VMEM((groups - 1, slot, width), bf16),
            pltpu.VMEM((all_rows, width), bf16),
            pltpu.VMEM((all_rows, width), bf16),
            pltpu.VMEM((slot, width), bf16),
            pltpu.VMEM((last_rows, columns), bf16),
            pltpu.VMEM((all_rows, units), bf16),
            pltpu.VMEM((units, width), f32),
            pltpu.VMEM((units, width), f32),
            pltpu.VMEM((units, width), f32),
            dma((7,)), dma((3,)), dma((chunks,)), dma((len(FIRST_X),)), dma((1,)), dma((2,)),
            dma((4 + len(LATE_D),)), dma((1 + half,)), pltpu.SemaphoreType.REGULAR,
        ],
        compiler_params=pltpu.CompilerParams(
            collective_id=0, has_side_effects=True, vmem_limit_bytes=LIMIT
        ),
    )(
        *(
            pltpu.with_memory_space_constraint(value, pltpu.HBM)
            for value in (
                expert_ids.reshape(1, count), route_weights.reshape(1, count),
                tokens, out_grad, w_gate_up, w_down, second_moment,
            )
        ),
    )
    return pl.pallas_call(
        final_kernel,
        out_shape=(
            jax.ShapeDtypeStruct((1, width, columns), bf16),
            jax.ShapeDtypeStruct((1, units, width), bf16),
        ),
        in_specs=[vmem_spec] * 4,
        out_specs=(any_spec, any_spec),
        scratch_shapes=[pltpu.VMEM((width, columns), bf16), dma((width // 256 + 1,))],
        compiler_params=pltpu.CompilerParams(vmem_limit_bytes=LIMIT),
    )(*held)


def solution(mesh):
    placed = (
        P(("wide", "narrow"), None),
        P(("wide", "narrow")),
        P(("wide", "narrow")),
        P(("wide", "narrow"), None),
        P(("wide", "narrow"), None, None),
        P(("wide", "narrow"), None, None),
        P(("wide", "narrow"), None, None),
    )
    return jax.shard_map(
        body,
        mesh=mesh,
        in_specs=placed,
        out_specs=(P(("wide", "narrow"), None, None), P(("wide", "narrow"), None, None)),
        check_vma=False,
    )
```

time: 29.9 us -> 28.5 us (0.953)
  Pallas kernels: 28.8 us -> 27.4 us
    pallas_call x1, Pallas kernels: 27.5 us -> 26.1 us  [body(): pl.pallas_call(functools.partial(kernel, groups, wides, slot, relayed), o...]
where the time goes in v1:
time: 28.5 us; the launch traced here: 28 us
  Pallas kernels  27.4 us (96%)
  between operations  0.64 us (2%)
    pallas_call x1, Pallas kernels, body(): pl.pallas_call(functools.partial(kernel, groups, wides, slot, relayed), o...  26.1 us
    pallas_call x1, Pallas kernels, body(): pl.pallas_call(final_kernel, out_shape=(jax.ShapeDtypeStruct((1, width, c...  1.26 us

profile of v1, /device:TPU:1, one launch (start us, length us, event | category | flops | bytes accessed | tf_op | source)
XLA Modules:
  0.0 28.0 jit_solution(238612648912371965)
XLA Ops:
  0.6 26.1 %shard_map.86 = (f32[2048,256]{1,0:T(8,128)S(1)}, bf16[2048,192]{1,0:T(8,128)(2,1)S(1)}, bf16[192,256]{1,0:T(8,128)(2,1)S(1)}, bf16[128,2048]{1,0:T(8,128)(2,1)S(1)}) custom-call(s32[1,128]{1,0:T(1,128)} %bitcast.2, f32[1,128]{1,0:T(1,128)} %bitcast.3, bf16[128,2048]{1,0:T(8,128)(2,1)} %tok_hbm.1, bf16[128,2048]{1,0:T(8,128)(2,1)} %og_hbm.1, ...), custom_call_target="tpu_custom_call" | custom-call | tf_op jit(solution)/shard_map/pallas_call | solution.py:425
  26.8 1.3 %shard_map.87 = (bf16[1,2048,256]{2,1,0:T(8,128)(2,1)}, bf16[1,128,2048]{2,1,0:T(8,128)(2,1)}) custom-call(f32[2048,256]{1,0:T(8,128)S(1)} %get-tuple-element.6.acc_p, bf16[2048,192]{1,0:T(8,128)(2,1)S(1)} %get-tuple-element.7.turned, bf16[192,256]{1,0:T(8,128)(2,1)S(1)} %get-tuple-element.8.pre_last, bf16[128,2048]{1,0:T(8,128)(2,1)S(1)} %get-tuple-element.9.update), custom_call_target="tpu_custom_call" | custom-call | tf_op jit(solution)/shard_map/pallas_call | solution.py:468

commit v2 on v1

--- a/solution.py
+++ b/solution.py
@@ -40,7 +40,7 @@
     groups, wides, slot, relayed,
     ids_hbm, rw_hbm, tok_hbm, og_hbm, wgu_hbm, wdn_hbm, sm_hbm,
     acc_p, turned, pre_last, ustage,
-    ids, rw, tok, og, wgu, wdn, sm, px, pd, rx, rd, lent, pre, hid, acc_d, moment, decay,
+    ids, rw, tok, og, wgu, wdn, sm, px, pd, rx, rd, lent, pre, hid, acc_d, moment, decay, turned_wdn,
     in_sem, send_sem, recv_sem, lent_sem, pass_sem, fsend_sem, frecv_sem, twice_sem, ready_sem,
 ):
     half = groups // 2
@@ -116,8 +116,17 @@
         value = kind * half + lax.rem(home + j, half)
         return jnp.logical_and(labels == value, slots == within)
 
-    def rows(b, h):
-        return pl.ds((2 * b + h) * slot, slot)
+    near = late[-1]
+    far = jnp.logical_and(wide == wides - 1, home > 0)
+    swapped = jnp.logical_and(wide == 0, home > 0)
+    near_swapped = jnp.logical_and(wide == 0, lax.rem(home + 1, half) > 0)
+    lent_swapped = jnp.logical_and(along(2) == 0, home > 0)
+
+    def rows(b, h, swap=None):
+        if swap is None or b not in (direct, near):
+            return pl.ds((2 * b + h) * slot, slot)
+        at = jnp.where(swap, direct + near - b, b)
+        return pl.ds(pl.multiple_of((2 * at + h) * slot, slot), slot)
 
     def remote(src, dst, s, r, dev):
         return pltpu.make_async_remote_copy(
@@ -127,7 +136,7 @@
 
     index, parts = {}, {}
     for b in range(1, groups):
-        widths = (DIAGONAL_X if b in diagonal else FIRST_X, EARLY_D if b in early else LATE_D)
+        widths = (DIAGONAL_X if b in diagonal else FIRST_X, EARLY_D if b in early[2:] else LATE_D)
         for a in (0, 1):
             parts[b, a] = spans(width, widths[a])
             for c in range(len(parts[b, a])):
@@ -141,7 +150,8 @@
         kind, j = order[b]
         cols = cols_of(b, a, c)
         return remote(
-            packed[a].at[b - 1, :, cols], received[a].at[rows(b, 0), cols],
+            packed[a].at[b - 1, :, cols],
+            received[a].at[rows(b, 0, far if b == direct else near_swapped), cols],
             send_sem.at[2 if a == 0 and b == direct and c < lends else a], recv_sem.at[index[b, a, c]], device(along(kind), peer(j)),
         )
 
@@ -157,7 +167,7 @@
     def hand_on(c):
         cols = cols_of(direct, 0, c)
         return remote(
-            lent.at[:, cols], rx.at[rows(direct, 0), cols],
+            lent.at[:, cols], rx.at[rows(direct, 0, lent_swapped), cols],
             pass_sem.at[0], recv_sem.at[index[direct, 0, c]], device(along(2), narrow),
         )
 
@@ -174,11 +184,14 @@
         else:
             send(direct, 0, c).start()
 
+    def go_direct():
+        for c in range(len(parts[direct, 1])):
+            send(direct, 1, c).start()
+
     def go_rest():
         for c in range(lends, len(FIRST_X)):
             send(direct, 0, c).start()
-        for c in range(len(parts[direct, 1])):
-            send(direct, 1, c).start()
+        pl.when(jnp.logical_not(far))(go_direct)
         for a in (0, 1):
             for b in diagonal:
                 for c in range(len(parts[b, a]) - a):
@@ -197,15 +210,16 @@
         kind, j = order[b]
         cols, other = cols_of(b, 1, final), 2 * lax.rem(home + j, half) + 1 - parity
         return remote(
-            pd.at[b - 1, :, cols], rd.at[rows(b, 1), cols],
+            pd.at[b - 1, :, cols], rd.at[rows(b, 1, near_swapped), cols],
             twice_sem.at[0], twice_sem.at[1 + b - half], device(along(kind), other),
         )
 
-    def forward(b, a, c):
+    def forward(b, a, c, late_one):
         cols = cols_of(b, a, c)
-        which = a if b < half else 2 + (b in beside) if a == 0 else 4 + c
+        x_sem = 0 if b < half else 2 + (b in beside)
+        which = (4 + c if late_one else 1) if a else x_sem
         return remote(
-            received[a].at[rows(b, 0), cols], received[a].at[rows(b, 1), cols],
+            received[a].at[rows(b, 0, swapped), cols], received[a].at[rows(b, 1, swapped), cols],
             fsend_sem.at[a], frecv_sem.at[which], sibling,
         )
 
@@ -265,6 +279,7 @@
     for b in beside:
         for c in range(len(parts[b, 1]) - (b in late)):
             send(b, 1, c).start()
+    pl.when(near_swapped)(send(near, 1, final).start)
     if half > 1:
         pl.semaphore_wait(ready_sem, half - 1)
     if relayed:
@@ -302,14 +317,14 @@
             [hidden_grad * factors[0], hidden_grad * factors[1]], axis=1
         ).astype(bf16)
 
-    def take(b, a, c):
+    def take(b, a, c, late_one):
         send(b, a, c).wait_recv()
-        forward(b, a, c).start()
+        forward(b, a, c, late_one).start()
 
     def take_all(blocks, a):
         for b in blocks:
             for c in range(len(parts[b, a])):
-                take(b, a, c)
+                take(b, a, c, False)
                 if relayed and (b, a, c) == (direct, 0, GATE):
                     pl.when(held_back)(go_rest)
 
@@ -317,15 +332,36 @@
     take_all([late[-1]], 0)
     settle(0, 0, half)
     settle(3, 0, 1)
+
+    def go_final(b):
+        send(b, 1, final).start()
+        send_twice(b).start()
+
+    for b in diagonal:
+        go_final(b)
+
+    @pl.when(jnp.logical_not(near_swapped))
+    def _():
+        go_final(near)
+
+    pl.when(far)(go_direct)
     first = pl.ds(0, half * 2 * slot)
     last = pl.ds(half * 2 * slot, half * 2 * slot)
     factors_first = project(first)
-    take_all(early[1:], 1)
-    for b in late:
-        send(b, 1, final).start()
-        send_twice(b).start()
+    take_all(early[2:], 1)
+    rest = pl.ds(*parts[near, 1][final])
+
+    @pl.when(jnp.logical_not(swapped))
+    def _():
+        take_all([direct], 1)
+
+    @pl.when(swapped)
+    def _():
+        take_all([near], 1)
+
     moment[...] = (0.95 / second_correction) * sm[...].astype(f32)
     decay[...] = 0.1 * wdn[...].astype(f32)
+    turned_wdn[...] = wdn[...].T
     settle(1, 1, half)
     finish(pre, first, mm(rd[first, :], wdn[...], ((1,), (1,))), factors_first)
     for i in range(width // 256):
@@ -333,6 +369,24 @@
         acc_p[cols, :] = mm(rx[first, cols], pre[first, :], ((0,), (0,)))
         acc_d[:, cols] = mm(hid[first, :], rd[first, cols], ((0,), (0,)))
     take_all(diagonal, 0)
+
+    def relay(c):
+        for b in diagonal:
+            take(b, 1, c, True)
+
+        @pl.when(jnp.logical_not(swapped))
+        def _():
+            take(near, 1, c, True)
+
+        @pl.when(swapped)
+        def _():
+            take(direct, 1, c, True)
+
+    @pl.when(parity == 1)
+    def _():
+        for c in range(final):
+            relay(c)
+
     settle(2, 0, half - 1)
     factors = project(last)
     turned[...] = rx[last, :].T
@@ -340,13 +394,9 @@
     hidden_grad = jnp.zeros((half * 2 * slot, hidden_units), f32)
     late_d = spans(width, LATE_D)
 
-    def relay(c):
-        for b in late:
-            take(b, 1, c)
-
     def add(c):
         cols = pl.ds(*late_d[c])
-        return hidden_grad + mm(rd[last, cols], wdn[:, cols], ((1,), (1,)))
+        return hidden_grad + mm(rd[last, cols], turned_wdn[cols, :], ((1,), (0,)))
 
     def update(c):
         cols = pl.ds(*late_d[c])
@@ -356,14 +406,28 @@
         ustage[:, cols] = (total / (root + 1e-08) + decay[:, cols]).astype(bf16)
 
     for c in range(final):
-        relay(c)
-    for c in range(final):
+
+        @pl.when(parity == 0)
+        def _():
+            relay(c)
+
         settle(4 + c, 1, half, pl.ds(*late_d[c]))
         hidden_grad = add(c)
         update(c)
-    for b in late:
+    for b in diagonal:
         send(b, 1, final).wait_recv()
         send_twice(b).wait_recv()
+
+    @pl.when(jnp.logical_not(swapped))
+    def _():
+        send(near, 1, final).wait_recv()
+        send_twice(near).wait_recv()
+
+    @pl.when(swapped)
+    def _():
+        take(direct, 1, final, True)
+        settle(4 + final, 1, 1, rest)
+
     hidden_grad = add(final)
     finish(pre_last, slice(None), hidden_grad, factors)
     update(final)
@@ -379,11 +443,21 @@
     part = rx.at[pl.ds(0, groups * slot)]
     remote(part, part, fsend_sem.at[0], frecv_sem.at[0], sibling).wait_send()
     part, cols = rd.at[pl.ds(0, groups * slot)], pl.ds(0, late_d[final][0])
-    rest = pl.ds(late_d[final][0], late_d[final][1])
     remote(part.at[:, cols], part.at[:, cols], fsend_sem.at[1], frecv_sem.at[0], sibling).wait_send()
     part = rd.at[pl.ds(0, half * slot), rest]
     remote(part, part, fsend_sem.at[1], frecv_sem.at[0], sibling).wait_send()
-    remote(part, part, twice_sem.at[0], frecv_sem.at[0], sibling).wait_send()
+    part = rd.at[pl.ds(0, slot), rest]
+
+    @pl.when(jnp.logical_not(near_swapped))
+    def _():
+        remote(part, part, twice_sem.at[0], frecv_sem.at[0], sibling).wait_send()
+
+    @pl.when(swapped)
+    def _():
+        remote(part, part, fsend_sem.at[1], frecv_sem.at[0], sibling).wait_send()
+
+    for _ in diagonal:
+        remote(part, part, twice_sem.at[0], frecv_sem.at[0], sibling).wait_send()
     if relayed:
 
         @pl.when(even)
@@ -450,6 +524,7 @@
             pltpu.VMEM((units, width), f32),
             pltpu.VMEM((units, width), f32),
             pltpu.VMEM((units, width), f32),
+            pltpu.VMEM((width, units), bf16),
             dma((7,)), dma((3,)), dma((chunks,)), dma((len(FIRST_X),)), dma((1,)), dma((2,)),
             dma((4 + len(LATE_D),)), dma((1 + half,)), pltpu.SemaphoreType.REGULAR,
         ],

time: 28.5 us -> 27.1 us (0.951)
  the two profiles are of different devices: /device:TPU:1 before, /device:TPU:5 now
where the time goes in v2:
time: 27.1 us; the launch traced here: 26.9 us
  Pallas kernels  26.3 us (97%)
  between operations  0.64 us (2%)
    pallas_call x1, Pallas kernels, body(): pl.pallas_call(functools.partial(kernel, groups, wides, slot, relayed), o...  25 us
    pallas_call x1, Pallas kernels, body(): pl.pallas_call(final_kernel, out_shape=(jax.ShapeDtypeStruct((1, width, c...  1.26 us

profile of v2, /device:TPU:5, one launch (start us, length us, event | category | flops | bytes accessed | tf_op | source)
XLA Modules:
  0.0 26.9 jit_solution(6527034091078761522)
XLA Ops:
  0.6 25.0 %shard_map.86 = (f32[2048,256]{1,0:T(8,128)S(1)}, bf16[2048,192]{1,0:T(8,128)(2,1)S(1)}, bf16[192,256]{1,0:T(8,128)(2,1)S(1)}, bf16[128,2048]{1,0:T(8,128)(2,1)S(1)}) custom-call(s32[1,128]{1,0:T(1,128)} %bitcast.2, f32[1,128]{1,0:T(1,128)} %bitcast.3, bf16[128,2048]{1,0:T(8,128)(2,1)} %tok_hbm.1, bf16[128,2048]{1,0:T(8,128)(2,1)} %og_hbm.1, ...), custom_call_target="tpu_custom_call" | custom-call | tf_op jit(solution)/shard_map/pallas_call | solution.py:499
  25.7 1.3 %shard_map.87 = (bf16[1,2048,256]{2,1,0:T(8,128)(2,1)}, bf16[1,128,2048]{2,1,0:T(8,128)(2,1)}) custom-call(f32[2048,256]{1,0:T(8,128)S(1)} %get-tuple-element.6.acc_p, bf16[2048,192]{1,0:T(8,128)(2,1)S(1)} %get-tuple-element.7.turned, bf16[192,256]{1,0:T(8,128)(2,1)S(1)} %get-tuple-element.8.pre_last, bf16[128,2048]{1,0:T(8,128)(2,1)S(1)} %get-tuple-element.9.update), custom_call_target="tpu_custom_call" | custom-call | tf_op jit(solution)/shard_map/pallas_call | solution.py:543

commit v3 on v2

--- a/solution.py
+++ b/solution.py
@@ -23,7 +23,7 @@
 PACK = (2, 3, 3)
 FIRST_X = (2, 3, 3)
 EARLY_D = (5, 3)
-DIAGONAL_X = (4, 4)
+DIAGONAL_X = (4, 2, 2)
 LATE_D = (2, 2, 2, 1, 1)
 
 
@@ -80,7 +80,11 @@
         )
     ):
         loads.append(pltpu.make_async_copy(src, dst, in_sem.at[i]))
-    for i in (5, 0, 6, 1):
+    pieces = spans(width, PACK)
+    for i, piece in enumerate(pieces):
+        cols = pl.ds(*piece)
+        loads.append(pltpu.make_async_copy(tok_hbm.at[:, cols], tok.at[:, cols], in_sem.at[7 + i]))
+    for i in [5] + list(range(7, 7 + len(pieces))) + [6, 1]:
         loads[i].start()
 
     barrier = pltpu.get_barrier_semaphore()
@@ -238,10 +242,8 @@
             else:
                 received[a][rows(0, 0), cols] = piece
 
-    loads[0].wait()
-    for i in (2, 3, 4):
-        loads[i].start()
-    for n, (start, size) in enumerate(spans(width, PACK)):
+    for n, (start, size) in enumerate(pieces):
+        loads[7 + n].wait()
         cols = pl.ds(start, size)
         store(0, cols, mm(chosen, tok[:, cols], ((1,), (0,))).astype(bf16))
         if n == 0:
@@ -266,6 +268,8 @@
         if n == 0:
             for j in range(1, half):
                 signal(ready_sem, device(wide, peer(j)))
+    for i in (2, 3, 4):
+        loads[i].start()
     loads[6].wait()
     weights = rw[...]
     weight = jnp.concatenate(
@@ -325,8 +329,8 @@
         for b in blocks:
             for c in range(len(parts[b, a])):
                 take(b, a, c, False)
-                if relayed and (b, a, c) == (direct, 0, GATE):
-                    pl.when(held_back)(go_rest)
+                if relayed and b == direct and a == 0 and c < 2:
+                    pl.when(jnp.logical_and(held_back, parity == c))(go_rest)
 
     take_all(early[1:], 0)
     take_all([late[-1]], 0)
@@ -381,16 +385,23 @@
         @pl.when(swapped)
         def _():
             take(direct, 1, c, True)
+            if c + 1 == final:
+                take(direct, 1, final, True)
 
     @pl.when(parity == 1)
     def _():
-        for c in range(final):
+        for c in range(final - 1):
             relay(c)
 
     settle(2, 0, half - 1)
     factors = project(last)
     turned[...] = rx[last, :].T
     turned_hid = hid[last, :].T
+
+    @pl.when(parity == 1)
+    def _():
+        relay(final - 1)
+
     hidden_grad = jnp.zeros((half * 2 * slot, hidden_units), f32)
     late_d = spans(width, LATE_D)
 
@@ -425,7 +436,6 @@
 
     @pl.when(swapped)
     def _():
-        take(direct, 1, final, True)
         settle(4 + final, 1, 1, rest)
 
     hidden_grad = add(final)
@@ -525,7 +535,7 @@
             pltpu.VMEM((units, width), f32),
             pltpu.VMEM((units, width), f32),
             pltpu.VMEM((width, units), bf16),
-            dma((7,)), dma((3,)), dma((chunks,)), dma((len(FIRST_X),)), dma((1,)), dma((2,)),
+            dma((7 + len(PACK),)), dma((3,)), dma((chunks,)), dma((len(FIRST_X),)), dma((1,)), dma((2,)),
             dma((4 + len(LATE_D),)), dma((1 + half,)), pltpu.SemaphoreType.REGULAR,
         ],
         compiler_params=pltpu.CompilerParams(

time: 27.1 us -> 26.4 us (0.974)
  the two profiles are of different devices: /device:TPU:5 before, /device:TPU:1 now
where the time goes in v3:
time: 26.4 us; the launch traced here: 26 us
  Pallas kernels  25.3 us (96%)
  between operations  0.64 us (2%)
    pallas_call x1, Pallas kernels, body(): pl.pallas_call(functools.partial(kernel, groups, wides, slot, relayed), o...  24.1 us
    pallas_call x1, Pallas kernels, body(): pl.pallas_call(final_kernel, out_shape=(jax.ShapeDtypeStruct((1, width, c...  1.26 us

profile of v3, /device:TPU:1, one launch (start us, length us, event | category | flops | bytes accessed | tf_op | source)
XLA Modules:
  0.0 26.0 jit_solution(14134550648352414695)
XLA Ops:
  0.6 24.1 %shard_map.86 = (f32[2048,256]{1,0:T(8,128)S(1)}, bf16[2048,192]{1,0:T(8,128)(2,1)S(1)}, bf16[192,256]{1,0:T(8,128)(2,1)S(1)}, bf16[128,2048]{1,0:T(8,128)(2,1)S(1)}) custom-call(s32[1,128]{1,0:T(1,128)} %bitcast.2, f32[1,128]{1,0:T(1,128)} %bitcast.3, bf16[128,2048]{1,0:T(8,128)(2,1)} %tok_hbm.1, bf16[128,2048]{1,0:T(8,128)(2,1)} %og_hbm.1, ...), custom_call_target="tpu_custom_call" | custom-call | tf_op jit(solution)/shard_map/pallas_call | solution.py:509
  24.7 1.3 %shard_map.87 = (bf16[1,2048,256]{2,1,0:T(8,128)(2,1)}, bf16[1,128,2048]{2,1,0:T(8,128)(2,1)}) custom-call(f32[2048,256]{1,0:T(8,128)S(1)} %get-tuple-element.6.acc_p, bf16[2048,192]{1,0:T(8,128)(2,1)S(1)} %get-tuple-element.7.turned, bf16[192,256]{1,0:T(8,128)(2,1)S(1)} %get-tuple-element.8.pre_last, bf16[128,2048]{1,0:T(8,128)(2,1)S(1)} %get-tuple-element.9.update), custom_call_target="tpu_custom_call" | custom-call | tf_op jit(solution)/shard_map/pallas_call | solution.py:553

commit v4 on v3

--- a/solution.py
+++ b/solution.py
@@ -17,9 +17,7 @@
     return lax.dot_general(a, b, (dims, ((), ())), preferred_element_type=f32)
 
 
-RELAYED = True
 LENDS = 2
-GATE = 1
 PACK = (2, 3, 3)
 FIRST_X = (2, 3, 3)
 EARLY_D = (5, 3)
@@ -41,7 +39,7 @@
     ids_hbm, rw_hbm, tok_hbm, og_hbm, wgu_hbm, wdn_hbm, sm_hbm,
     acc_p, turned, pre_last, ustage,
     ids, rw, tok, og, wgu, wdn, sm, px, pd, rx, rd, lent, pre, hid, acc_d, moment, decay, turned_wdn,
-    in_sem, send_sem, recv_sem, lent_sem, pass_sem, fsend_sem, frecv_sem, twice_sem, ready_sem,
+    in_sem, sent_sem, recv_sem, lent_sem, frecv_sem, twice_sem, ready_sem,
 ):
     half = groups // 2
     width = tok.shape[1]
@@ -57,12 +55,23 @@
     def device(w, n):
         return {"wide": w, "narrow": n}
 
-    def peer(j):
-        return 2 * lax.rem(home + j, half) + parity
+    def peer(j, other=0):
+        return 2 * lax.rem(home + j, half) + lax.rem(parity + other, 2)
+
+    def crossed(step, j):
+        same = jnp.logical_and(along(step) == 0, lax.rem(home + j, half) == 0)
+        return jnp.where(same, 0, 1)
+
+    def target(step, j, other=0):
+        return device(along(step), peer(j, crossed(step, j) + other))
+
+    def source(step, j):
+        return device(along(step), peer(j, crossed(0, 0)))
 
     odd = lax.rem(wide, 2) == 1
     even = jnp.logical_not(odd)
     sibling = device(wide, 2 * home + 1 - parity)
+    leads = parity != crossed(0, 0)
 
     order = [(0, 0), (1, 0)] + [(0, j) for j in range(2, half)]
     order += [(1, j) for j in range(1, half)] + [(0, 1)]
@@ -72,29 +81,32 @@
     diagonal = [b for b in late if order[b][0]]
     beside = [b for b in range(1, groups) if not order[b][0]]
 
-    loads = []
-    for i, (src, dst) in enumerate(
-        (
-            (tok_hbm, tok), (og_hbm, og), (wgu_hbm.at[0], wgu), (wdn_hbm.at[0], wdn),
-            (sm_hbm.at[0], sm), (ids_hbm, ids), (rw_hbm, rw),
-        )
-    ):
-        loads.append(pltpu.make_async_copy(src, dst, in_sem.at[i]))
     pieces = spans(width, PACK)
-    for i, piece in enumerate(pieces):
-        cols = pl.ds(*piece)
-        loads.append(pltpu.make_async_copy(tok_hbm.at[:, cols], tok.at[:, cols], in_sem.at[7 + i]))
-    for i in [5] + list(range(7, 7 + len(pieces))) + [6, 1]:
-        loads[i].start()
+    loads = {}
+
+    def load(name, src, dst, i):
+        loads[name] = pltpu.make_async_copy(src, dst, in_sem.at[i])
+
+    load("ids", ids_hbm, ids, 0)
+    for n, piece in enumerate(pieces):
+        load(n, tok_hbm.at[:, pl.ds(*piece)], tok.at[:, pl.ds(*piece)], 6 + n)
+    load("rw", rw_hbm, rw, 1)
+    load("og", og_hbm, og, 2)
+    for copy in loads.values():
+        copy.start()
+    load("wgu", wgu_hbm.at[0], wgu, 3)
+    load("wdn", wdn_hbm.at[0], wdn, 4)
+    load("sm", sm_hbm.at[0], sm, 5)
 
     barrier = pltpu.get_barrier_semaphore()
 
     def signal(sem, partner):
         pl.semaphore_signal(sem, inc=1, device_id=partner, device_id_type=pl.DeviceIdType.MESH)
 
-    signal(barrier, device(along(-1), narrow))
+    signal(barrier, source(-1, 0))
     for j in range(1, half):
-        signal(barrier, device(wide, peer(j)))
+        signal(barrier, source(0, j))
+        signal(barrier, device(wide, peer(j, crossed(0, 0) + 1)))
     signal(barrier, sibling)
     if relayed:
 
@@ -102,7 +114,7 @@
         def _():
             signal(barrier, device(along(1), narrow))
 
-    loads[5].wait()
+    loads["ids"].wait()
     count = tok.shape[0]
     labels = ids[...]
     pad_groups = max(8, groups)
@@ -124,6 +136,7 @@
     far = jnp.logical_and(wide == wides - 1, home > 0)
     swapped = jnp.logical_and(wide == 0, home > 0)
     near_swapped = jnp.logical_and(wide == 0, lax.rem(home + 1, half) > 0)
+    plain = jnp.logical_and(wide == 0, home == 0)
     lent_swapped = jnp.logical_and(along(2) == 0, home > 0)
 
     def rows(b, h, swap=None):
@@ -138,25 +151,32 @@
             device_id=dev, device_id_type=pl.DeviceIdType.MESH,
         )
 
-    index, parts = {}, {}
+    index, parts, used = {}, {}, 0
     for b in range(1, groups):
         widths = (DIAGONAL_X if b in diagonal else FIRST_X, EARLY_D if b in early[2:] else LATE_D)
         for a in (0, 1):
             parts[b, a] = spans(width, widths[a])
+            one = b in beside if a == 0 else b in early
             for c in range(len(parts[b, a])):
-                index[b, a, c] = len(index)
+                index[b, a, c] = used if one else used + c
+            used += 1 if one else len(parts[b, a])
+
     packed, received = (px, pd), (rx, rd)
 
     def cols_of(b, a, c):
         return pl.ds(*parts[b, a][c])
 
+    def slot_of(b, a, c, swap):
+        if a and b in (direct, near):
+            return jnp.where(swap, index[direct + near - b, 1, c], index[b, 1, c])
+        return index[b, a, c]
+
     def send(b, a, c):
         kind, j = order[b]
-        cols = cols_of(b, a, c)
+        cols, swap = cols_of(b, a, c), far if b == direct else near_swapped
         return remote(
-            packed[a].at[b - 1, :, cols],
-            received[a].at[rows(b, 0, far if b == direct else near_swapped), cols],
-            send_sem.at[2 if a == 0 and b == direct and c < lends else a], recv_sem.at[index[b, a, c]], device(along(kind), peer(j)),
+            packed[a].at[b - 1, :, cols], received[a].at[rows(b, 0, swap), cols],
+            sent_sem.at[0], recv_sem.at[slot_of(b, a, c, swap)], target(kind, j),
         )
 
     lends = LENDS if relayed else 0
@@ -165,14 +185,14 @@
         cols = cols_of(direct, 0, c)
         return remote(
             px.at[direct - 1, :, cols], lent.at[:, cols],
-            send_sem.at[2], lent_sem.at[c], device(along(-1), narrow),
+            sent_sem.at[0], lent_sem.at[c], device(along(-1), narrow),
         )
 
     def hand_on(c):
         cols = cols_of(direct, 0, c)
         return remote(
             lent.at[:, cols], rx.at[rows(direct, 0, lent_swapped), cols],
-            pass_sem.at[0], recv_sem.at[index[direct, 0, c]], device(along(2), narrow),
+            sent_sem.at[0], recv_sem.at[index[direct, 0, c]], target(2, 0),
         )
 
     def go_first(c):
@@ -201,10 +221,6 @@
                 for c in range(len(parts[b, a]) - a):
                     send(b, a, c).start()
 
-    def first_sent():
-        part = px.at[0, :, pl.ds(0, first_columns)]
-        remote(part, part, send_sem.at[2], recv_sem.at[0], sibling).wait_send()
-
     held_back = jnp.logical_and(odd, wide != wides - 1)
     first_columns = sum(FIRST_X[:lends]) * width // sum(FIRST_X)
 
@@ -212,24 +228,23 @@
 
     def send_twice(b):
         kind, j = order[b]
-        cols, other = cols_of(b, 1, final), 2 * lax.rem(home + j, half) + 1 - parity
+        cols = cols_of(b, 1, final)
         return remote(
             pd.at[b - 1, :, cols], rd.at[rows(b, 1, near_swapped), cols],
-            twice_sem.at[0], twice_sem.at[1 + b - half], device(along(kind), other),
+            sent_sem.at[0], twice_sem.at[0], target(kind, j, 1),
         )
 
-    def forward(b, a, c, late_one):
-        cols = cols_of(b, a, c)
-        x_sem = 0 if b < half else 2 + (b in beside)
-        which = (4 + c if late_one else 1) if a else x_sem
+    def forward(b, a, cols, which):
         return remote(
             received[a].at[rows(b, 0, swapped), cols], received[a].at[rows(b, 1, swapped), cols],
-            fsend_sem.at[a], frecv_sem.at[which], sibling,
+            sent_sem.at[0], frecv_sem.at[which], sibling,
         )
 
+    def arrived(part, sem):
+        return remote(part, part, sent_sem.at[0], sem, sibling)
+
     def settle(which, a, blocks, cols=slice(None)):
-        part = received[a].at[pl.ds(0, blocks * slot), cols]
-        remote(part, part, fsend_sem.at[a], frecv_sem.at[which], sibling).wait_recv()
+        arrived(received[a].at[pl.ds(0, blocks * slot), cols], frecv_sem.at[which]).wait_recv()
 
     selects = [select_of(b) for b in range(groups)]
     chosen = jnp.concatenate([s.astype(f32) for s in selects], axis=0).astype(bf16)
@@ -243,22 +258,22 @@
                 received[a][rows(0, 0), cols] = piece
 
     for n, (start, size) in enumerate(pieces):
-        loads[7 + n].wait()
+        loads[n].wait()
         cols = pl.ds(start, size)
         store(0, cols, mm(chosen, tok[:, cols], ((1,), (0,))).astype(bf16))
         if n == 0:
-            near = 1 + half - 1 + 1
+            entered = 1 + 2 * (half - 1) + 1
             if relayed:
 
                 @pl.when(odd)
                 def _():
-                    pl.semaphore_wait(barrier, near + 1)
+                    pl.semaphore_wait(barrier, entered + 1)
 
                 @pl.when(even)
                 def _():
-                    pl.semaphore_wait(barrier, near)
+                    pl.semaphore_wait(barrier, entered)
             else:
-                pl.semaphore_wait(barrier, near)
+                pl.semaphore_wait(barrier, entered)
         for c, (at, extent) in enumerate(spans(width, FIRST_X)):
             if at + extent == start + size:
                 if c < lends:
@@ -268,14 +283,14 @@
         if n == 0:
             for j in range(1, half):
                 signal(ready_sem, device(wide, peer(j)))
-    for i in (2, 3, 4):
-        loads[i].start()
-    loads[6].wait()
+    for name in ("wgu", "wdn", "sm"):
+        loads[name].start()
+    loads["rw"].wait()
+    loads["og"].wait()
     weights = rw[...]
     weight = jnp.concatenate(
         [jnp.sum(jnp.where(s, weights, 0.0), axis=1, keepdims=True) for s in selects], axis=0
     )
-    loads[1].wait()
     for start, size in spans(width, PACK):
         cols = pl.ds(start, size)
         placed = mm(chosen, og[:, cols], ((1,), (0,)))
@@ -291,14 +306,7 @@
     else:
         go_rest()
     for a in (0, 1):
-        whole = received[a]
-        remote(
-            whole.at[rows(0, 0)], whole.at[rows(0, 1)],
-            fsend_sem.at[a], frecv_sem.at[a], sibling,
-        ).start()
-    loads[2].wait()
-    loads[3].wait()
-    loads[4].wait()
+        forward(0, a, slice(None), a).start()
     if relayed:
 
         @pl.when(even)
@@ -321,28 +329,36 @@
             [hidden_grad * factors[0], hidden_grad * factors[1]], axis=1
         ).astype(bf16)
 
-    def take(b, a, c, late_one):
-        send(b, a, c).wait_recv()
-        forward(b, a, c, late_one).start()
-
-    def take_all(blocks, a):
-        for b in blocks:
-            for c in range(len(parts[b, a])):
-                take(b, a, c, False)
-                if relayed and b == direct and a == 0 and c < 2:
-                    pl.when(jnp.logical_and(held_back, parity == c))(go_rest)
-
-    take_all(early[1:], 0)
-    take_all([late[-1]], 0)
-    settle(0, 0, half)
-    settle(3, 0, 1)
+    def take(b, a, c, which):
+        cols = cols_of(b, a, c)
+        i = index[near if b == direct and a and which > 2 else b, a, c]
+        arrived(received[a].at[rows(b, 0, swapped), cols], recv_sem.at[i]).wait_recv()
+        forward(b, a, cols, which).start()
+
+    def take_whole(b, a, which):
+        i = index[direct if b == near and a else b, a, 0]
+        arrived(received[a].at[rows(b, 0, swapped)], recv_sem.at[i]).wait_recv()
+        forward(b, a, slice(None), which).start()
+
+    for c in range(len(FIRST_X)):
+        take(direct, 0, c, 0)
+        if relayed and c < 2:
+            ready = leads if c else jnp.logical_not(leads)
+            pl.when(jnp.logical_and(held_back, ready))(go_rest)
+    for b in beside:
+        take_whole(b, 0, 0)
+    settle(0, 0, half + 1)
+
+    def single(b):
+        return jnp.logical_and(wide == wides - 1, lax.rem(home + order[b][1], half) == 0)
 
     def go_final(b):
         send(b, 1, final).start()
         send_twice(b).start()
 
     for b in diagonal:
-        go_final(b)
+        send(b, 1, final).start()
+        pl.when(jnp.logical_not(single(b)))(send_twice(b).start)
 
     @pl.when(jnp.logical_not(near_swapped))
     def _():
@@ -351,17 +367,20 @@
     pl.when(far)(go_direct)
     first = pl.ds(0, half * 2 * slot)
     last = pl.ds(half * 2 * slot, half * 2 * slot)
+    for name in ("wgu", "wdn", "sm"):
+        loads[name].wait()
     factors_first = project(first)
-    take_all(early[2:], 1)
     rest = pl.ds(*parts[near, 1][final])
+    for b in early[2:]:
+        take_whole(b, 1, 1)
 
     @pl.when(jnp.logical_not(swapped))
     def _():
-        take_all([direct], 1)
+        take_whole(direct, 1, 1)
 
     @pl.when(swapped)
     def _():
-        take_all([near], 1)
+        take_whole(near, 1, 1)
 
     moment[...] = (0.95 / second_correction) * sm[...].astype(f32)
     decay[...] = 0.1 * wdn[...].astype(f32)
@@ -372,23 +391,27 @@
         cols = pl.ds(i * 256, 256)
         acc_p[cols, :] = mm(rx[first, cols], pre[first, :], ((0,), (0,)))
         acc_d[:, cols] = mm(hid[first, :], rd[first, cols], ((0,), (0,)))
-    take_all(diagonal, 0)
+    for b in diagonal:
+        for c in range(len(DIAGONAL_X)):
+            take(b, 0, c, 2)
 
     def relay(c):
         for b in diagonal:
-            take(b, 1, c, True)
+            take(b, 1, c, 3 + c)
+            if c + 1 == final:
+                pl.when(plain)(lambda b=b: take(b, 1, final, 3 + final))
 
         @pl.when(jnp.logical_not(swapped))
         def _():
-            take(near, 1, c, True)
+            take(near, 1, c, 3 + c)
 
         @pl.when(swapped)
         def _():
-            take(direct, 1, c, True)
+            take(direct, 1, c, 3 + c)
             if c + 1 == final:
-                take(direct, 1, final, True)
-
-    @pl.when(parity == 1)
+                take(direct, 1, final, 3 + final)
+
+    @pl.when(leads)
     def _():
         for c in range(final - 1):
             relay(c)
@@ -398,7 +421,7 @@
     turned[...] = rx[last, :].T
     turned_hid = hid[last, :].T
 
-    @pl.when(parity == 1)
+    @pl.when(leads)
     def _():
         relay(final - 1)
 
@@ -418,72 +441,70 @@
 
     for c in range(final):
 
-        @pl.when(parity == 0)
+        @pl.when(jnp.logical_not(leads))
         def _():
             relay(c)
 
-        settle(4 + c, 1, half, pl.ds(*late_d[c]))
+        settle(3 + c, 1, half, pl.ds(*late_d[c]))
         hidden_grad = add(c)
         update(c)
-    for b in diagonal:
-        send(b, 1, final).wait_recv()
-        send_twice(b).wait_recv()
+    tail = rd.at[pl.ds(0, slot), rest]
+
+    @pl.when(jnp.logical_not(plain))
+    def _():
+        for b in diagonal:
+            arrived(tail, recv_sem.at[index[b, 1, final]]).wait_recv()
+
+    pl.when(plain)(lambda: settle(3 + final, 1, half - 1, rest))
 
     @pl.when(jnp.logical_not(swapped))
     def _():
-        send(near, 1, final).wait_recv()
-        send_twice(near).wait_recv()
+        arrived(tail, recv_sem.at[index[near, 1, final]]).wait_recv()
 
     @pl.when(swapped)
     def _():
-        settle(4 + final, 1, 1, rest)
-
+        settle(3 + final, 1, 1, rest)
+
+    def doubled(blocks, condition):
+        @pl.when(condition)
+        def _():
+            arrived(rd.at[pl.ds(0, blocks * slot), rest], twice_sem.at[0]).wait_recv()
+
+    ordinary = jnp.logical_not(jnp.logical_or(plain, swapped))
+    doubled(half, ordinary)
+    doubled(1, plain)
+    if half > 1:
+        doubled(half - 1, swapped)
     hidden_grad = add(final)
     finish(pre_last, slice(None), hidden_grad, factors)
     update(final)
-    part = px.at[1:]
-    remote(part, part, send_sem.at[0], recv_sem.at[0], sibling).wait_send()
+    def sent(part):
+        arrived(part, recv_sem.at[0]).wait_send()
+
+    most = pl.ds(0, late_d[final][0])
+    sent(px)
+    sent(pd)
+    sent(rx.at[pl.ds(0, groups * slot)])
+    sent(rd.at[pl.ds(0, groups * slot), most])
+    sent(rd.at[pl.ds(0, half * slot), rest])
+    for b in diagonal:
+        pl.when(jnp.logical_not(single(b)))(lambda: sent(tail))
+        pl.when(plain)(lambda: sent(tail))
+    unless_near = jnp.logical_not(near_swapped)
+    pl.when(unless_near)(lambda: sent(tail))
+    pl.when(swapped)(lambda: sent(tail))
     if relayed:
-        first_sent()
-        part = px.at[0, :, pl.ds(first_columns, width - first_columns)]
-        remote(part, part, send_sem.at[0], recv_sem.at[0], sibling).wait_send()
-    else:
-        remote(px.at[0], px.at[0], send_sem.at[0], recv_sem.at[0], sibling).wait_send()
-    remote(pd, pd, send_sem.at[1], recv_sem.at[0], sibling).wait_send()
-    part = rx.at[pl.ds(0, groups * slot)]
-    remote(part, part, fsend_sem.at[0], frecv_sem.at[0], sibling).wait_send()
-    part, cols = rd.at[pl.ds(0, groups * slot)], pl.ds(0, late_d[final][0])
-    remote(part.at[:, cols], part.at[:, cols], fsend_sem.at[1], frecv_sem.at[0], sibling).wait_send()
-    part = rd.at[pl.ds(0, half * slot), rest]
-    remote(part, part, fsend_sem.at[1], frecv_sem.at[0], sibling).wait_send()
-    part = rd.at[pl.ds(0, slot), rest]
-
-    @pl.when(jnp.logical_not(near_swapped))
-    def _():
-        remote(part, part, twice_sem.at[0], frecv_sem.at[0], sibling).wait_send()
-
-    @pl.when(swapped)
-    def _():
-        remote(part, part, fsend_sem.at[1], frecv_sem.at[0], sibling).wait_send()
-
-    for _ in diagonal:
-        remote(part, part, twice_sem.at[0], frecv_sem.at[0], sibling).wait_send()
-    if relayed:
-
-        @pl.when(even)
-        def _():
-            part = lent.at[:, pl.ds(0, first_columns)]
-            remote(part, part, pass_sem.at[0], recv_sem.at[0], sibling).wait_send()
+        pl.when(even)(lambda: sent(lent.at[:, pl.ds(0, first_columns)]))
 
 
 def final_kernel(acc_p, turned, pre_last, update, gout, uout, gstage, out_sem):
     tiles = acc_p.shape[0] // 256
-    outs = [pltpu.make_async_copy(update, uout.at[0], out_sem.at[tiles])]
+    outs = [pltpu.make_async_copy(update, uout.at[0], out_sem.at[0])]
     outs[0].start()
     for i in range(tiles):
         r = pl.ds(i * 256, 256)
         gstage[r, :] = (acc_p[r, :] + mm(turned[r, :], pre_last[...], ((1,), (0,)))).astype(bf16)
-        copy = pltpu.make_async_copy(gstage.at[r], gout.at[0, r], out_sem.at[i])
+        copy = pltpu.make_async_copy(gstage.at[r], gout.at[0, r], out_sem.at[0])
         copy.start()
         outs.append(copy)
     for copy in outs:
@@ -501,8 +522,8 @@
     half = groups // 2
     all_rows = groups * 2 * slot
     last_rows = half * 2 * slot
-    relayed = RELAYED and wides % 2 == 0 and wides >= 4
-    chunks = (groups - 1) * (len(FIRST_X) + len(LATE_D))
+    relayed = wides % 2 == 0 and wides >= 4
+    chunks = len(FIRST_X) + half + half - 1 + (half - 1) * len(DIAGONAL_X) + half * len(LATE_D)
     dma = pltpu.SemaphoreType.DMA
     any_spec = pl.BlockSpec(memory_space=pl.ANY)
     vmem_spec = pl.BlockSpec(memory_space=pltpu.VMEM)
@@ -535,8 +556,8 @@
             pltpu.VMEM((units, width), f32),
             pltpu.VMEM((units, width), f32),
             pltpu.VMEM((width, units), bf16),
-            dma((7 + len(PACK),)), dma((3,)), dma((chunks,)), dma((len(FIRST_X),)), dma((1,)), dma((2,)),
-            dma((4 + len(LATE_D),)), dma((1 + half,)), pltpu.SemaphoreType.REGULAR,
+            dma((6 + len(PACK),)), dma((1,)), dma((chunks,)), dma((max(LENDS, 1),)),
+            dma((3 + len(LATE_D),)), dma((1,)), pltpu.SemaphoreType.REGULAR,
         ],
         compiler_params=pltpu.CompilerParams(
             collective_id=0, has_side_effects=True, vmem_limit_bytes=LIMIT
@@ -558,7 +579,7 @@
         ),
         in_specs=[vmem_spec] * 4,
         out_specs=(any_spec, any_spec),
-        scratch_shapes=[pltpu.VMEM((width, columns), bf16), dma((width // 256 + 1,))],
+        scratch_shapes=[pltpu.VMEM((width, columns), bf16), dma((1,))],
         compiler_params=pltpu.CompilerParams(vmem_limit_bytes=LIMIT),
     )(*held)
 

time: 26.4 us -> 25.8 us (0.977); the launches traced: 26 us -> 25.7 us
  Pallas kernels: 25.3 us -> 25 us
where the time goes in v4:
time: 25.8 us; the launch traced here: 25.7 us
  Pallas kernels  25 us (97%)
  between operations  0.64 us (2%)
    pallas_call x1, Pallas kernels, body(): pl.pallas_call(functools.partial(kernel, groups, wides, slot, relayed), o...  23.9 us
    pallas_call x1, Pallas kernels, body(): pl.pallas_call(final_kernel, out_shape=(jax.ShapeDtypeStruct((1, width, c...  1.19 us

profile of v4, /device:TPU:1, one launch (start us, length us, event | category | flops | bytes accessed | tf_op | source)
XLA Modules:
  0.0 25.7 jit_solution(14764086442505833778)
XLA Ops:
  0.6 23.9 %shard_map.86 = (f32[2048,256]{1,0:T(8,128)S(1)}, bf16[2048,192]{1,0:T(8,128)(2,1)S(1)}, bf16[192,256]{1,0:T(8,128)(2,1)S(1)}, bf16[128,2048]{1,0:T(8,128)(2,1)S(1)}) custom-call(s32[1,128]{1,0:T(1,128)} %bitcast.2, f32[1,128]{1,0:T(1,128)} %bitcast.3, bf16[128,2048]{1,0:T(8,128)(2,1)} %tok_hbm.1, bf16[128,2048]{1,0:T(8,128)(2,1)} %og_hbm.1, ...), custom_call_target="tpu_custom_call" | custom-call | tf_op jit(solution)/shard_map/pallas_call | solution.py:530
  24.5 1.2 %shard_map.87 = (bf16[1,2048,256]{2,1,0:T(8,128)(2,1)}, bf16[1,128,2048]{2,1,0:T(8,128)(2,1)}) custom-call(f32[2048,256]{1,0:T(8,128)S(1)} %get-tuple-element.6.acc_p, bf16[2048,192]{1,0:T(8,128)(2,1)S(1)} %get-tuple-element.7.turned, bf16[192,256]{1,0:T(8,128)(2,1)S(1)} %get-tuple-element.8.pre_last, bf16[128,2048]{1,0:T(8,128)(2,1)S(1)} %get-tuple-element.9.update), custom_call_target="tpu_custom_call" | custom-call | tf_op jit(solution)/shard_map/pallas_call | solution.py:574

commit v5 on v4

--- a/solution.py
+++ b/solution.py
@@ -18,11 +18,13 @@
 
 
 LENDS = 2
+AHEAD = 1
+TURN = 1
 PACK = (2, 3, 3)
 FIRST_X = (2, 3, 3)
 EARLY_D = (5, 3)
 DIAGONAL_X = (4, 2, 2)
-LATE_D = (2, 2, 2, 1, 1)
+LATE_D = (3, 2, 2, 1)
 
 
 def spans(width, weights):
@@ -39,7 +41,7 @@
     ids_hbm, rw_hbm, tok_hbm, og_hbm, wgu_hbm, wdn_hbm, sm_hbm,
     acc_p, turned, pre_last, ustage,
     ids, rw, tok, og, wgu, wdn, sm, px, pd, rx, rd, lent, pre, hid, acc_d, moment, decay, turned_wdn,
-    in_sem, sent_sem, recv_sem, lent_sem, frecv_sem, twice_sem, ready_sem,
+    in_sem, sent_sem, recv_sem, lent_sem, frecv_sem, ready_sem,
 ):
     half = groups // 2
     width = tok.shape[1]
@@ -74,7 +76,7 @@
     leads = parity != crossed(0, 0)
 
     order = [(0, 0), (1, 0)] + [(0, j) for j in range(2, half)]
-    order += [(1, j) for j in range(1, half)] + [(0, 1)]
+    order += [(0, 1)] + [(1, j) for j in range(1, half)]
     early = list(range(half))
     late = list(range(half, groups))
     direct = 1
@@ -132,11 +134,10 @@
         value = kind * half + lax.rem(home + j, half)
         return jnp.logical_and(labels == value, slots == within)
 
-    near = late[-1]
+    near = half
     far = jnp.logical_and(wide == wides - 1, home > 0)
     swapped = jnp.logical_and(wide == 0, home > 0)
     near_swapped = jnp.logical_and(wide == 0, lax.rem(home + 1, half) > 0)
-    plain = jnp.logical_and(wide == 0, home == 0)
     lent_swapped = jnp.logical_and(along(2) == 0, home > 0)
 
     def rows(b, h, swap=None):
@@ -212,27 +213,23 @@
         for c in range(len(parts[direct, 1])):
             send(direct, 1, c).start()
 
-    def go_rest():
+    def go_more():
         for c in range(lends, len(FIRST_X)):
             send(direct, 0, c).start()
+
+    held_back = jnp.logical_and(odd, wide != wides - 1) if relayed else wide < 0
+
+    def go_rest():
+        pl.when(held_back)(go_more)
         pl.when(jnp.logical_not(far))(go_direct)
         for a in (0, 1):
             for b in diagonal:
-                for c in range(len(parts[b, a]) - a):
+                for c in range(len(parts[b, a])):
                     send(b, a, c).start()
 
-    held_back = jnp.logical_and(odd, wide != wides - 1)
     first_columns = sum(FIRST_X[:lends]) * width // sum(FIRST_X)
 
-    final = len(LATE_D) - 1
-
-    def send_twice(b):
-        kind, j = order[b]
-        cols = cols_of(b, 1, final)
-        return remote(
-            pd.at[b - 1, :, cols], rd.at[rows(b, 1, near_swapped), cols],
-            sent_sem.at[0], twice_sem.at[0], target(kind, j, 1),
-        )
+    final = len(LATE_D)
 
     def forward(b, a, cols, which):
         return remote(
@@ -283,6 +280,7 @@
         if n == 0:
             for j in range(1, half):
                 signal(ready_sem, device(wide, peer(j)))
+    pl.when(jnp.logical_not(held_back))(go_more)
     for name in ("wgu", "wdn", "sm"):
         loads[name].start()
     loads["rw"].wait()
@@ -296,9 +294,8 @@
         placed = mm(chosen, og[:, cols], ((1,), (0,)))
         store(1, cols, (weight * placed).astype(bf16))
     for b in beside:
-        for c in range(len(parts[b, 1]) - (b in late)):
+        for c in range(len(parts[b, 1])):
             send(b, 1, c).start()
-    pl.when(near_swapped)(send(near, 1, final).start)
     if half > 1:
         pl.semaphore_wait(ready_sem, half - 1)
     if relayed:
@@ -348,29 +345,15 @@
     for b in beside:
         take_whole(b, 0, 0)
     settle(0, 0, half + 1)
-
-    def single(b):
-        return jnp.logical_and(wide == wides - 1, lax.rem(home + order[b][1], half) == 0)
-
-    def go_final(b):
-        send(b, 1, final).start()
-        send_twice(b).start()
-
-    for b in diagonal:
-        send(b, 1, final).start()
-        pl.when(jnp.logical_not(single(b)))(send_twice(b).start)
-
-    @pl.when(jnp.logical_not(near_swapped))
-    def _():
-        go_final(near)
-
     pl.when(far)(go_direct)
-    first = pl.ds(0, half * 2 * slot)
-    last = pl.ds(half * 2 * slot, half * 2 * slot)
+    pair = 2 * slot
+    first, last = pl.ds(0, half * pair), pl.ds(half * pair, half * pair)
+    soon, rest_rows = pl.ds(0, (half + 1) * pair), pl.ds((half + 1) * pair, (half - 1) * pair)
     for name in ("wgu", "wdn", "sm"):
         loads[name].wait()
-    factors_first = project(first)
-    rest = pl.ds(*parts[near, 1][final])
+    factors_soon = project(soon)
+    factors_first = [factor[: half * pair] for factor in factors_soon]
+    factors = [factor[half * pair :] for factor in factors_soon]
     for b in early[2:]:
         take_whole(b, 1, 1)
 
@@ -398,8 +381,6 @@
     def relay(c):
         for b in diagonal:
             take(b, 1, c, 3 + c)
-            if c + 1 == final:
-                pl.when(plain)(lambda b=b: take(b, 1, final, 3 + final))
 
         @pl.when(jnp.logical_not(swapped))
         def _():
@@ -408,8 +389,6 @@
         @pl.when(swapped)
         def _():
             take(direct, 1, c, 3 + c)
-            if c + 1 == final:
-                take(direct, 1, final, 3 + final)
 
     @pl.when(leads)
     def _():
@@ -417,8 +396,10 @@
             relay(c)
 
     settle(2, 0, half - 1)
-    factors = project(last)
-    turned[...] = rx[last, :].T
+    if half > 1:
+        factors = [
+            jnp.concatenate(both, axis=0) for both in zip(factors, project(rest_rows), strict=True)
+        ]
     turned_hid = hid[last, :].T
 
     @pl.when(leads)
@@ -439,60 +420,28 @@
         root = second * lax.rsqrt(second)
         ustage[:, cols] = (total / (root + 1e-08) + decay[:, cols]).astype(bf16)
 
+    follows = jnp.logical_not(leads)
+    if AHEAD:
+        pl.when(follows)(lambda: relay(0))
     for c in range(final):
-
-        @pl.when(jnp.logical_not(leads))
-        def _():
-            relay(c)
+        if c + AHEAD < final:
+            pl.when(follows)(lambda c=c: relay(c + AHEAD))
 
         settle(3 + c, 1, half, pl.ds(*late_d[c]))
         hidden_grad = add(c)
+        if c + 1 == final:
+            finish(pre_last, slice(None), hidden_grad, factors)
         update(c)
-    tail = rd.at[pl.ds(0, slot), rest]
-
-    @pl.when(jnp.logical_not(plain))
-    def _():
-        for b in diagonal:
-            arrived(tail, recv_sem.at[index[b, 1, final]]).wait_recv()
-
-    pl.when(plain)(lambda: settle(3 + final, 1, half - 1, rest))
-
-    @pl.when(jnp.logical_not(swapped))
-    def _():
-        arrived(tail, recv_sem.at[index[near, 1, final]]).wait_recv()
-
-    @pl.when(swapped)
-    def _():
-        settle(3 + final, 1, 1, rest)
-
-    def doubled(blocks, condition):
-        @pl.when(condition)
-        def _():
-            arrived(rd.at[pl.ds(0, blocks * slot), rest], twice_sem.at[0]).wait_recv()
-
-    ordinary = jnp.logical_not(jnp.logical_or(plain, swapped))
-    doubled(half, ordinary)
-    doubled(1, plain)
-    if half > 1:
-        doubled(half - 1, swapped)
-    hidden_grad = add(final)
-    finish(pre_last, slice(None), hidden_grad, factors)
-    update(final)
+        if c == TURN:
+            turned[...] = rx[last, :].T
+
     def sent(part):
         arrived(part, recv_sem.at[0]).wait_send()
 
-    most = pl.ds(0, late_d[final][0])
     sent(px)
     sent(pd)
     sent(rx.at[pl.ds(0, groups * slot)])
-    sent(rd.at[pl.ds(0, groups * slot), most])
-    sent(rd.at[pl.ds(0, half * slot), rest])
-    for b in diagonal:
-        pl.when(jnp.logical_not(single(b)))(lambda: sent(tail))
-        pl.when(plain)(lambda: sent(tail))
-    unless_near = jnp.logical_not(near_swapped)
-    pl.when(unless_near)(lambda: sent(tail))
-    pl.when(swapped)(lambda: sent(tail))
+    sent(rd.at[pl.ds(0, groups * slot)])
     if relayed:
         pl.when(even)(lambda: sent(lent.at[:, pl.ds(0, first_columns)]))
 
@@ -557,7 +506,7 @@
             pltpu.VMEM((units, width), f32),
             pltpu.VMEM((width, units), bf16),
             dma((6 + len(PACK),)), dma((1,)), dma((chunks,)), dma((max(LENDS, 1),)),
-            dma((3 + len(LATE_D),)), dma((1,)), pltpu.SemaphoreType.REGULAR,
+            dma((3 + len(LATE_D),)), pltpu.SemaphoreType.REGULAR,
         ],
         compiler_params=pltpu.CompilerParams(
             collective_id=0, has_side_effects=True, vmem_limit_bytes=LIMIT

time: 25.8 us -> 25.7 us (level)
  no operation moved by 1% of the time
where the time goes in v5:
time: 25.7 us; the launch traced here: 25.6 us
  Pallas kernels  25 us (97%)
  between operations  0.64 us (2%)
    pallas_call x1, Pallas kernels, body(): pl.pallas_call(functools.partial(kernel, groups, wides, slot, relayed), o...  23.8 us
    pallas_call x1, Pallas kernels, body(): pl.pallas_call(final_kernel, out_shape=(jax.ShapeDtypeStruct((1, width, c...  1.19 us

profile of v5, /device:TPU:1, one launch (start us, length us, event | category | flops | bytes accessed | tf_op | source)
XLA Modules:
  0.0 25.6 jit_solution(10233598321428249575)
XLA Ops:
  0.6 23.8 %shard_map.86 = (f32[2048,256]{1,0:T(8,128)S(1)}, bf16[2048,192]{1,0:T(8,128)(2,1)S(1)}, bf16[192,256]{1,0:T(8,128)(2,1)S(1)}, bf16[128,2048]{1,0:T(8,128)(2,1)S(1)}) custom-call(s32[1,128]{1,0:T(1,128)} %bitcast.2, f32[1,128]{1,0:T(1,128)} %bitcast.3, bf16[128,2048]{1,0:T(8,128)(2,1)} %tok_hbm.1, bf16[128,2048]{1,0:T(8,128)(2,1)} %og_hbm.1, ...), custom_call_target="tpu_custom_call" | custom-call | tf_op jit(solution)/shard_map/pallas_call | solution.py:479
  24.4 1.2 %shard_map.87 = (bf16[1,2048,256]{2,1,0:T(8,128)(2,1)}, bf16[1,128,2048]{2,1,0:T(8,128)(2,1)}) custom-call(f32[2048,256]{1,0:T(8,128)S(1)} %get-tuple-element.6.acc_p, bf16[2048,192]{1,0:T(8,128)(2,1)S(1)} %get-tuple-element.7.turned, bf16[192,256]{1,0:T(8,128)(2,1)S(1)} %get-tuple-element.8.pre_last, bf16[128,2048]{1,0:T(8,128)(2,1)S(1)} %get-tuple-element.9.update), custom_call_target="tpu_custom_call" | custom-call | tf_op jit(solution)/shard_map/pallas_call | solution.py:523

commit v6 on v5

--- a/solution.py
+++ b/solution.py
@@ -41,7 +41,7 @@
     ids_hbm, rw_hbm, tok_hbm, og_hbm, wgu_hbm, wdn_hbm, sm_hbm,
     acc_p, turned, pre_last, ustage,
     ids, rw, tok, og, wgu, wdn, sm, px, pd, rx, rd, lent, pre, hid, acc_d, moment, decay, turned_wdn,
-    in_sem, sent_sem, recv_sem, lent_sem, frecv_sem, ready_sem,
+    in_sem, sent_sem, recv_sem, lent_sem, frecv_sem, ready_sem, pair_sem,
 ):
     half = groups // 2
     width = tok.shape[1]
@@ -64,11 +64,8 @@
         same = jnp.logical_and(along(step) == 0, lax.rem(home + j, half) == 0)
         return jnp.where(same, 0, 1)
 
-    def target(step, j, other=0):
-        return device(along(step), peer(j, crossed(step, j) + other))
-
-    def source(step, j):
-        return device(along(step), peer(j, crossed(0, 0)))
+    def target(step, j, a):
+        return device(along(step), peer(j, crossed(step, j) if a else 0))
 
     odd = lax.rem(wide, 2) == 1
     even = jnp.logical_not(odd)
@@ -105,10 +102,9 @@
     def signal(sem, partner):
         pl.semaphore_signal(sem, inc=1, device_id=partner, device_id_type=pl.DeviceIdType.MESH)
 
-    signal(barrier, source(-1, 0))
+    signal(barrier, device(along(-1), narrow))
     for j in range(1, half):
-        signal(barrier, source(0, j))
-        signal(barrier, device(wide, peer(j, crossed(0, 0) + 1)))
+        signal(barrier, device(wide, peer(j)))
     signal(barrier, sibling)
     if relayed:
 
@@ -140,11 +136,10 @@
     near_swapped = jnp.logical_and(wide == 0, lax.rem(home + 1, half) > 0)
     lent_swapped = jnp.logical_and(along(2) == 0, home > 0)
 
-    def rows(b, h, swap=None):
-        if swap is None or b not in (direct, near):
-            return pl.ds((2 * b + h) * slot, slot)
-        at = jnp.where(swap, direct + near - b, b)
-        return pl.ds(pl.multiple_of((2 * at + h) * slot, slot), slot)
+    def rows(b, h, swap):
+        at = jnp.where(swap, direct + near - b, b) if b in (direct, near) else b
+        start = (2 * at + h) * slot
+        return pl.ds(start if isinstance(start, int) else pl.multiple_of(start, slot), slot)
 
     def remote(src, dst, s, r, dev):
         return pltpu.make_async_remote_copy(
@@ -176,8 +171,9 @@
         kind, j = order[b]
         cols, swap = cols_of(b, a, c), far if b == direct else near_swapped
         return remote(
-            packed[a].at[b - 1, :, cols], received[a].at[rows(b, 0, swap), cols],
-            sent_sem.at[0], recv_sem.at[slot_of(b, a, c, swap)], target(kind, j),
+            packed[a].at[b - 1, :, cols],
+            received[a].at[rows(b, crossed(kind, j) if a else 0, swap), cols],
+            sent_sem.at[0], recv_sem.at[slot_of(b, a, c, swap)], target(kind, j, a),
         )
 
     lends = LENDS if relayed else 0
@@ -193,7 +189,7 @@
         cols = cols_of(direct, 0, c)
         return remote(
             lent.at[:, cols], rx.at[rows(direct, 0, lent_swapped), cols],
-            sent_sem.at[0], recv_sem.at[index[direct, 0, c]], target(2, 0),
+            sent_sem.at[0], recv_sem.at[index[direct, 0, c]], target(2, 0, 0),
         )
 
     def go_first(c):
@@ -231,9 +227,14 @@
 
     final = len(LATE_D)
 
+    def heard(b, a):
+        return crossed(0, 0) if a and b else 0
+
     def forward(b, a, cols, which):
+        h = heard(b, a)
         return remote(
-            received[a].at[rows(b, 0, swapped), cols], received[a].at[rows(b, 1, swapped), cols],
+            received[a].at[rows(b, h, swapped), cols],
+            received[a].at[rows(b, 1 - h, swapped), cols],
             sent_sem.at[0], frecv_sem.at[which], sibling,
         )
 
@@ -252,14 +253,14 @@
             if b:
                 packed[a][b - 1, :, cols] = piece
             else:
-                received[a][rows(0, 0), cols] = piece
+                received[a][rows(0, 0, swapped), cols] = piece
 
     for n, (start, size) in enumerate(pieces):
         loads[n].wait()
         cols = pl.ds(start, size)
         store(0, cols, mm(chosen, tok[:, cols], ((1,), (0,))).astype(bf16))
         if n == 0:
-            entered = 1 + 2 * (half - 1) + 1
+            entered = 1 + half - 1 + 1
             if relayed:
 
                 @pl.when(odd)
@@ -293,11 +294,13 @@
         cols = pl.ds(start, size)
         placed = mm(chosen, og[:, cols], ((1,), (0,)))
         store(1, cols, (weight * placed).astype(bf16))
+    if half > 1:
+        pl.semaphore_wait(ready_sem, half - 1)
+    signal(pair_sem, sibling)
+    pl.semaphore_wait(pair_sem, 1)
     for b in beside:
         for c in range(len(parts[b, 1])):
             send(b, 1, c).start()
-    if half > 1:
-        pl.semaphore_wait(ready_sem, half - 1)
     if relayed:
         pl.when(jnp.logical_not(held_back))(go_rest)
     else:
@@ -329,19 +332,18 @@
     def take(b, a, c, which):
         cols = cols_of(b, a, c)
         i = index[near if b == direct and a and which > 2 else b, a, c]
-        arrived(received[a].at[rows(b, 0, swapped), cols], recv_sem.at[i]).wait_recv()
+        arrived(received[a].at[rows(b, heard(b, a), swapped), cols], recv_sem.at[i]).wait_recv()
         forward(b, a, cols, which).start()
 
     def take_whole(b, a, which):
         i = index[direct if b == near and a else b, a, 0]
-        arrived(received[a].at[rows(b, 0, swapped)], recv_sem.at[i]).wait_recv()
+        arrived(received[a].at[rows(b, heard(b, a), swapped)], recv_sem.at[i]).wait_recv()
         forward(b, a, slice(None), which).start()
 
     for c in range(len(FIRST_X)):
         take(direct, 0, c, 0)
         if relayed and c < 2:
-            ready = leads if c else jnp.logical_not(leads)
-            pl.when(jnp.logical_and(held_back, ready))(go_rest)
+            pl.when(jnp.logical_and(held_back, parity == c))(go_rest)
     for b in beside:
         take_whole(b, 0, 0)
     settle(0, 0, half + 1)
@@ -506,7 +508,7 @@
             pltpu.VMEM((units, width), f32),
             pltpu.VMEM((width, units), bf16),
             dma((6 + len(PACK),)), dma((1,)), dma((chunks,)), dma((max(LENDS, 1),)),
-            dma((3 + len(LATE_D),)), pltpu.SemaphoreType.REGULAR,
+            dma((3 + len(LATE_D),)), pltpu.SemaphoreType.REGULAR, pltpu.SemaphoreType.REGULAR,
         ],
         compiler_params=pltpu.CompilerParams(
             collective_id=0, has_side_effects=True, vmem_limit_bytes=LIMIT

time: 25.7 us -> 25.3 us (0.984)
  Pallas kernels: 25 us -> 24.5 us
    pallas_call x1, Pallas kernels: 23.8 us -> 23.3 us  [body(): pl.pallas_call(functools.partial(kernel, groups, wides, slot, relayed), o...]
where the time goes in v6:
time: 25.3 us; the launch traced here: 25.1 us
  Pallas kernels  24.5 us (97%)
  between operations  0.64 us (3%)
    pallas_call x1, Pallas kernels, body(): pl.pallas_call(functools.partial(kernel, groups, wides, slot, relayed), o...  23.3 us
    pallas_call x1, Pallas kernels, body(): pl.pallas_call(final_kernel, out_shape=(jax.ShapeDtypeStruct((1, width, c...  1.18 us

profile of v6, /device:TPU:1, one launch (start us, length us, event | category | flops | bytes accessed | tf_op | source)
XLA Modules:
  0.0 25.1 jit_solution(7161745195767574877)
XLA Ops:
  0.6 23.3 %shard_map.86 = (f32[2048,256]{1,0:T(8,128)S(1)}, bf16[2048,192]{1,0:T(8,128)(2,1)S(1)}, bf16[192,256]{1,0:T(8,128)(2,1)S(1)}, bf16[128,2048]{1,0:T(8,128)(2,1)S(1)}) custom-call(s32[1,128]{1,0:T(1,128)} %bitcast.2, f32[1,128]{1,0:T(1,128)} %bitcast.3, bf16[128,2048]{1,0:T(8,128)(2,1)} %tok_hbm.1, bf16[128,2048]{1,0:T(8,128)(2,1)} %og_hbm.1, ...), custom_call_target="tpu_custom_call" | custom-call | tf_op jit(solution)/shard_map/pallas_call | solution.py:481
  23.9 1.2 %shard_map.87 = (bf16[1,2048,256]{2,1,0:T(8,128)(2,1)}, bf16[1,128,2048]{2,1,0:T(8,128)(2,1)}) custom-call(f32[2048,256]{1,0:T(8,128)S(1)} %get-tuple-element.6.acc_p, bf16[2048,192]{1,0:T(8,128)(2,1)S(1)} %get-tuple-element.7.turned, bf16[192,256]{1,0:T(8,128)(2,1)S(1)} %get-tuple-element.8.pre_last, bf16[128,2048]{1,0:T(8,128)(2,1)S(1)} %get-tuple-element.9.update), custom_call_target="tpu_custom_call" | custom-call | tf_op jit(solution)/shard_map/pallas_call | solution.py:525

commit v7 on v6

--- a/solution.py
+++ b/solution.py
@@ -18,12 +18,12 @@
 
 
 LENDS = 2
-AHEAD = 1
+AHEAD = 2
 TURN = 1
 PACK = (2, 3, 3)
 FIRST_X = (2, 3, 3)
 EARLY_D = (5, 3)
-DIAGONAL_X = (4, 2, 2)
+DIAGONAL_X = (4, 4)
 LATE_D = (3, 2, 2, 1)
 
 
@@ -423,8 +423,8 @@
         ustage[:, cols] = (total / (root + 1e-08) + decay[:, cols]).astype(bf16)
 
     follows = jnp.logical_not(leads)
-    if AHEAD:
-        pl.when(follows)(lambda: relay(0))
+    for c in range(AHEAD):
+        pl.when(follows)(lambda c=c: relay(c))
     for c in range(final):
         if c + AHEAD < final:
             pl.when(follows)(lambda c=c: relay(c + AHEAD))

time: 25.3 us -> 25.1 us (level)
  no operation moved by 1% of the time
where the time goes in v7:
time: 25.1 us; the launch traced here: 25 us
  Pallas kernels  24.3 us (97%)
  between operations  0.64 us (3%)
    pallas_call x1, Pallas kernels, body(): pl.pallas_call(functools.partial(kernel, groups, wides, slot, relayed), o...  23.2 us
    pallas_call x1, Pallas kernels, body(): pl.pallas_call(final_kernel, out_shape=(jax.ShapeDtypeStruct((1, width, c...  1.18 us

profile of v7, /device:TPU:1, one launch (start us, length us, event | category | flops | bytes accessed | tf_op | source)
XLA Modules:
  0.0 25.0 jit_solution(11658166476457121042)
XLA Ops:
  0.6 23.2 %shard_map.86 = (f32[2048,256]{1,0:T(8,128)S(1)}, bf16[2048,192]{1,0:T(8,128)(2,1)S(1)}, bf16[192,256]{1,0:T(8,128)(2,1)S(1)}, bf16[128,2048]{1,0:T(8,128)(2,1)S(1)}) custom-call(s32[1,128]{1,0:T(1,128)} %bitcast.2, f32[1,128]{1,0:T(1,128)} %bitcast.3, bf16[128,2048]{1,0:T(8,128)(2,1)} %tok_hbm.1, bf16[128,2048]{1,0:T(8,128)(2,1)} %og_hbm.1, ...), custom_call_target="tpu_custom_call" | custom-call | tf_op jit(solution)/shard_map/pallas_call | solution.py:481
  23.8 1.2 %shard_map.87 = (bf16[1,2048,256]{2,1,0:T(8,128)(2,1)}, bf16[1,128,2048]{2,1,0:T(8,128)(2,1)}) custom-call(f32[2048,256]{1,0:T(8,128)S(1)} %get-tuple-element.6.acc_p, bf16[2048,192]{1,0:T(8,128)(2,1)S(1)} %get-tuple-element.7.turned, bf16[192,256]{1,0:T(8,128)(2,1)S(1)} %get-tuple-element.8.pre_last, bf16[128,2048]{1,0:T(8,128)(2,1)S(1)} %get-tuple-element.9.update), custom_call_target="tpu_custom_call" | custom-call | tf_op jit(solution)/shard_map/pallas_call | solution.py:525

commit v8 on v7

--- a/solution.py
+++ b/solution.py
@@ -88,14 +88,14 @@
 
     load("ids", ids_hbm, ids, 0)
     for n, piece in enumerate(pieces):
-        load(n, tok_hbm.at[:, pl.ds(*piece)], tok.at[:, pl.ds(*piece)], 6 + n)
-    load("rw", rw_hbm, rw, 1)
+        load(n, tok_hbm.at[:, pl.ds(*piece)], tok.at[:, pl.ds(*piece)], 1 if n == 0 else 4)
+    load("rw", rw_hbm, rw, 0)
     load("og", og_hbm, og, 2)
     for copy in loads.values():
         copy.start()
     load("wgu", wgu_hbm.at[0], wgu, 3)
-    load("wdn", wdn_hbm.at[0], wdn, 4)
-    load("sm", sm_hbm.at[0], sm, 5)
+    load("wdn", wdn_hbm.at[0], wdn, 3)
+    load("sm", sm_hbm.at[0], sm, 3)
 
     barrier = pltpu.get_barrier_semaphore()
 
@@ -112,7 +112,8 @@
         def _():
             signal(barrier, device(along(1), narrow))
 
-    loads["ids"].wait()
+    both = acc_d.at[pl.ds(0, 2), pl.ds(0, tok.shape[0])]
+    pltpu.make_async_copy(both, both, in_sem.at[0]).wait()
     count = tok.shape[0]
     labels = ids[...]
     pad_groups = max(8, groups)
@@ -256,7 +257,10 @@
                 received[a][rows(0, 0, swapped), cols] = piece
 
     for n, (start, size) in enumerate(pieces):
-        loads[n].wait()
+        if n < 2:
+            late_cols = pl.ds(pieces[n][0], (width if n else pieces[1][0]) - pieces[n][0])
+            part = tok.at[:, late_cols]
+            pltpu.make_async_copy(part, part, in_sem.at[4 if n else 1]).wait()
         cols = pl.ds(start, size)
         store(0, cols, mm(chosen, tok[:, cols], ((1,), (0,))).astype(bf16))
         if n == 0:
@@ -284,7 +288,6 @@
     pl.when(jnp.logical_not(held_back))(go_more)
     for name in ("wgu", "wdn", "sm"):
         loads[name].start()
-    loads["rw"].wait()
     loads["og"].wait()
     weights = rw[...]
     weight = jnp.concatenate(
@@ -351,8 +354,7 @@
     pair = 2 * slot
     first, last = pl.ds(0, half * pair), pl.ds(half * pair, half * pair)
     soon, rest_rows = pl.ds(0, (half + 1) * pair), pl.ds((half + 1) * pair, (half - 1) * pair)
-    for name in ("wgu", "wdn", "sm"):
-        loads[name].wait()
+    pltpu.make_async_copy(acc_p, acc_p, in_sem.at[3]).wait()
     factors_soon = project(soon)
     factors_first = [factor[: half * pair] for factor in factors_soon]
     factors = [factor[half * pair :] for factor in factors_soon]
@@ -507,7 +509,7 @@
             pltpu.VMEM((units, width), f32),
             pltpu.VMEM((units, width), f32),
             pltpu.VMEM((width, units), bf16),
-            dma((6 + len(PACK),)), dma((1,)), dma((chunks,)), dma((max(LENDS, 1),)),
+            dma((5,)), dma((1,)), dma((chunks,)), dma((LENDS,)),
             dma((3 + len(LATE_D),)), pltpu.SemaphoreType.REGULAR, pltpu.SemaphoreType.REGULAR,
         ],
         compiler_params=pltpu.CompilerParams(

time: 25.1 us -> 25.2 us (level)
  no operation moved by 1% of the time
where the time goes in v8:
time: 25.2 us; the launch traced here: 25 us
  Pallas kernels  24.4 us (97%)
  between operations  0.64 us (3%)
    pallas_call x1, Pallas kernels, body(): pl.pallas_call(functools.partial(kernel, groups, wides, slot, relayed), o...  23.2 us
    pallas_call x1, Pallas kernels, body(): pl.pallas_call(final_kernel, out_shape=(jax.ShapeDtypeStruct((1, width, c...  1.19 us

profile of v8, /device:TPU:1, one launch (start us, length us, event | category | flops | bytes accessed | tf_op | source)
XLA Modules:
  0.0 25.0 jit_solution(15903805611317678885)
XLA Ops:
  0.6 23.2 %shard_map.86 = (f32[2048,256]{1,0:T(8,128)S(1)}, bf16[2048,192]{1,0:T(8,128)(2,1)S(1)}, bf16[192,256]{1,0:T(8,128)(2,1)S(1)}, bf16[128,2048]{1,0:T(8,128)(2,1)S(1)}) custom-call(s32[1,128]{1,0:T(1,128)} %bitcast.2, f32[1,128]{1,0:T(1,128)} %bitcast.3, bf16[128,2048]{1,0:T(8,128)(2,1)} %tok_hbm.1, bf16[128,2048]{1,0:T(8,128)(2,1)} %og_hbm.1, ...), custom_call_target="tpu_custom_call" | custom-call | tf_op jit(solution)/shard_map/pallas_call | solution.py:483
  23.8 1.2 %shard_map.87 = (bf16[1,2048,256]{2,1,0:T(8,128)(2,1)}, bf16[1,128,2048]{2,1,0:T(8,128)(2,1)}) custom-call(f32[2048,256]{1,0:T(8,128)S(1)} %get-tuple-element.6.acc_p, bf16[2048,192]{1,0:T(8,128)(2,1)S(1)} %get-tuple-element.7.turned, bf16[192,256]{1,0:T(8,128)(2,1)S(1)} %get-tuple-element.8.pre_last, bf16[128,2048]{1,0:T(8,128)(2,1)S(1)} %get-tuple-element.9.update), custom_call_target="tpu_custom_call" | custom-call | tf_op jit(solution)/shard_map/pallas_call | solution.py:527
